TPU v7x, 512 devices: a whole 4x4x16 slice. The times are simulated.
512 devices in a mesh: member: 8 (over z_lo), node: 64 (over y, z_hi, x, core).
Axes of the slice: x: 4, y: 4, z: 16 (z_hi: 2, z_lo: 8; z = z_hi * 8 + z_lo), core: 2. Of those that a mesh axis runs over, the one named last changes fastest.
Arguments:
- vertex_embedding_array: bfloat16 [8, 262144, 128], P('member', 'node'), may hold values from -12 to 12
- result_sensitivity: bfloat16 [8, 262144, 128], P('member', 'node'), may hold values from -6 to 6
- hidden_projection: bfloat16 [128, 128], replicated, may hold values from -0.5 to 0.5
- aggregate_projection: bfloat16 [128, 128], replicated, may hold values from -0.5 to 0.5
- aggregate_offset: float32 [128], replicated, may hold values from -3 to 3
- assignment_projection: bfloat16 [16, 32], replicated, may hold values from -1.5 to 1.5
- softmax_sharpness: float32 [8], replicated, may hold values from 0.5 to 2
- state_asking_map: bfloat16 [16, 16], replicated, may hold values from -1.5 to 1.5
- state_lookup_map: bfloat16 [16, 16], replicated, may hold values from -1.5 to 1.5
- state_content_map: bfloat16 [16, 16], replicated, may hold values from -1.5 to 1.5
- result_projection: bfloat16 [128, 128], replicated, may hold values from -0.5 to 0.5
Outputs:
- vertex_sensitivity: float32 [8, 262144, 128], P('member', 'node')
- mid_grad: float32 [128, 128], replicated
- feature_grad: float32 [128, 128], replicated
- bias_grad: float32 [128], replicated
- slice_grad: float32 [16, 32], replicated
- temperature_grad: float32 [8], replicated
- query_grad: float32 [16, 16], replicated
- key_grad: float32 [16, 16], replicated
- value_grad: float32 [16, 16], replicated
- projection_grad: float32 [128, 128], replicated
All inputs are finite; a program needn't handle non-finite values.
Results may differ from a plain program's by a relative error of at most 0.0054.
The roundings to bfloat16 on the way count: a program that leaves them out, or rounds other values in their place, can miss the bound.
Values sent between devices are 32-bit elements; how exact they have to be, the bound alone decides.
No kernel may reach another device: no remote copies, remote signals or barrier semaphores. Data moves between devices by JAX's collectives and lax.ppermute only.
A program may use at most 64 MiB of HBM per device.

v0:
```python
import math

import jax
import jax.numpy as jnp
from jax import lax
from jax.sharding import PartitionSpec as P

MODEL_WIDTH = 128
NUM_CHANNELS = 8
D = 16


epsilon = 1e-05


def attend(physical_state_vectors, state_asking_map, state_lookup_map, state_content_map):
    exact_arithmetic_mode = lax.Precision.HIGHEST
    asking_vectors = jnp.einsum(
        "uzi,ib->uzb", physical_state_vectors, state_asking_map, precision=exact_arithmetic_mode
    )
    random_seed_list = jnp.einsum(
        "uzi,ib->uzb", physical_state_vectors, state_lookup_map, precision=exact_arithmetic_mode
    )
    content_vectors = jnp.einsum(
        "uzi,ib->uzb", physical_state_vectors, state_content_map, precision=exact_arithmetic_mode
    )
    assignment_shares = jnp.einsum(
        "hme,hke->hmk", asking_vectors, random_seed_list, precision=exact_arithmetic_mode
    ) / math.sqrt(physical_state_vectors.shape[-1])
    expon = jnp.exp(assignment_shares)
    attention_rows = expon / jnp.sum(expon, -1, keepdims=True)
    return jnp.einsum(
        "lso,log->lsg", attention_rows, content_vectors, precision=exact_arithmetic_mode
    )


def shards(
    vertex_embedding_array,
    result_sensitivity,
    hidden_projection,
    aggregate_projection,
    aggregate_offset,
    assignment_projection,
    softmax_sharpness,
    state_asking_map,
    state_lookup_map,
    state_content_map,
    result_projection,
):
    channel_embedding = vertex_embedding_array[0]
    incoming_sensitivity = result_sensitivity[0]
    mesh_node_rows = channel_embedding.shape[0]
    mid_half = (
        jnp.dot(channel_embedding, hidden_projection, preferred_element_type=jnp.float32)
        .astype(jnp.bfloat16)
        .reshape(mesh_node_rows, NUM_CHANNELS, D)
    )
    feature_halfway = (
        (
            jnp.dot(channel_embedding, aggregate_projection, preferred_element_type=jnp.float32)
            + aggregate_offset
        )
        .astype(jnp.bfloat16)
        .reshape(mesh_node_rows, NUM_CHANNELS, D)
    )
    assignment_shares = jnp.einsum(
        "nhd,dm->nhm", mid_half, assignment_projection, preferred_element_type=jnp.float32
    )
    assignment_energies = assignment_shares / softmax_sharpness[None, :, None]
    expon = jnp.exp(assignment_energies)
    probs = expon / jnp.sum(expon, -1, keepdims=True)
    probability_halfway = probs.astype(jnp.bfloat16)
    pooled_numerator = jnp.einsum(
        "wou,wog->oug", probability_halfway, feature_halfway, preferred_element_type=jnp.float32
    )
    denominator = jnp.sum(probs, 0)
    pooled_numerator, denominator = lax.psum((pooled_numerator, denominator), "node")
    physical_state_vectors = pooled_numerator / (denominator[:, :, None] + epsilon)
    token_out, attend_back = jax.vjp(
        attend,
        physical_state_vectors,
        state_asking_map.astype(jnp.float32),
        state_lookup_map.astype(jnp.float32),
        state_content_map.astype(jnp.float32),
    )
    tokens_halfway = token_out.astype(jnp.bfloat16)
    mixed_half = (
        jnp.einsum(
            "afq,fqx->afx", probability_halfway, tokens_halfway, preferred_element_type=jnp.float32
        )
        .reshape(mesh_node_rows, MODEL_WIDTH)
        .astype(jnp.bfloat16)
    )
    backward_halfway = (
        jnp.dot(incoming_sensitivity, result_projection.T, preferred_element_type=jnp.float32)
        .astype(jnp.bfloat16)
        .reshape(mesh_node_rows, NUM_CHANNELS, D)
    )
    mapping_contribution = jnp.dot(
        mixed_half.T, incoming_sensitivity, preferred_element_type=jnp.float32
    )
    slice_token_gradient = jnp.einsum(
        "wou,wog->oug", probability_halfway, backward_halfway, preferred_element_type=jnp.float32
    )
    slice_token_gradient = lax.psum(slice_token_gradient, "node")
    piece_reverse_derivative, asking_contribution, lookup_contribution, content_contribution = (
        attend_back(slice_token_gradient)
    )
    inverse = 1.0 / (denominator + epsilon)
    numerator_halfway = (piece_reverse_derivative * inverse[:, :, None]).astype(jnp.bfloat16)
    denom_back = -jnp.sum(piece_reverse_derivative * physical_state_vectors, -1) * inverse
    probability_backward = jnp.einsum(
        "yrq,req->yre", backward_halfway, tokens_halfway, preferred_element_type=jnp.float32
    )
    probability_backward = probability_backward + jnp.einsum(
        "yrq,req->yre", feature_halfway, numerator_halfway, preferred_element_type=jnp.float32
    )
    probability_backward = probability_backward + denom_back[None]
    feature_backward = jnp.einsum(
        "afq,fqx->afx", probability_halfway, numerator_halfway, preferred_element_type=jnp.float32
    ).reshape(mesh_node_rows, MODEL_WIDTH)
    shift_term_derivative = jnp.sum(feature_backward, 0)
    feat_back_half = feature_backward.astype(jnp.bfloat16)
    inner = jnp.sum(probs * probability_backward, -1, keepdims=True)
    assignment_energy_adjoint = probs * (probability_backward - inner)
    inverse_spread_derivative = (
        -jnp.sum(assignment_energy_adjoint * assignment_energies, axis=(0, 2)) / softmax_sharpness
    )
    assignment_partial_result = (
        assignment_energy_adjoint / softmax_sharpness[None, :, None]
    ).astype(jnp.bfloat16)
    division_term_derivative = jnp.einsum(
        "nhd,nhm->dm", mid_half, assignment_partial_result, preferred_element_type=jnp.float32
    )
    mid_back_half = (
        jnp.einsum(
            "nhm,dm->nhd",
            assignment_partial_result,
            assignment_projection,
            preferred_element_type=jnp.float32,
        )
        .reshape(mesh_node_rows, MODEL_WIDTH)
        .astype(jnp.bfloat16)
    )
    hidden_contribution = jnp.dot(
        channel_embedding.T, mid_back_half, preferred_element_type=jnp.float32
    )
    channel_contribution = jnp.dot(
        channel_embedding.T, feat_back_half, preferred_element_type=jnp.float32
    )
    vertex_sensitivity = jnp.dot(
        mid_back_half, hidden_projection.T, preferred_element_type=jnp.float32
    ) + jnp.dot(feat_back_half, aggregate_projection.T, preferred_element_type=jnp.float32)
    dominant_summands = (hidden_contribution, channel_contribution, mapping_contribution)
    trailing_summands = (shift_term_derivative, division_term_derivative, inverse_spread_derivative)
    token_terms = (asking_contribution, lookup_contribution, content_contribution)
    piece_totals = lax.psum((token_terms[0], token_terms[1], token_terms[2]), "member")
    totalled = lax.psum(dominant_summands + trailing_summands, ("member", "node"))
    large_sums = totalled[:3]
    small_sums = totalled[3:]
    return (
        vertex_sensitivity[None],
        large_sums[0],
        large_sums[1],
        small_sums[0],
        small_sums[1],
        small_sums[2],
        piece_totals[0],
        piece_totals[1],
        piece_totals[2],
        large_sums[2],
    )


def solution(mesh):
    placed = (
        P("member", "node", None),
        P("member", "node", None),
        P(),
        P(),
        P(),
        P(),
        P(),
        P(),
        P(),
        P(),
        P(),
    )
    return jax.shard_map(
        shards,
        mesh=mesh,
        in_specs=placed,
        out_specs=(P("member", "node", None), P(), P(), P(), P(), P(), P(), P(), P(), P()),
        check_vma=False,
    )
```

profile of v0, /device:TPU:1, one launch (start us, length us, event | category | flops | bytes accessed | tf_op | source)
XLA Modules:
  0.0 1062.4 jit_solution(12174903163778519607)
XLA Ops:
  7.3 1.1 copy-done
  8.4 1.2 convolution_convert_fusion.3
  9.7 0.5 fusion.6
  10.2 0.4 convolution_convert_fusion.2
  10.7 1.1 exponential_reduce_fusion
  11.8 1.0 fusion.31
  12.8 0.9 copy-done.10
  13.8 0.7 fusion.37
  14.4 0.7 fusion.35
  15.1 558.1 %all-reduce.2 = (f32[8,32,16]{1,2,0:T(8,128)}, f32[8,32]{1,0:T(8,128)S(1)}, f32[8,32,16]{1,2,0:T(8,128)S(1)}) all-reduce(f32[8,32,16]{1,2,0:T(8,128)S(1)} %fusion.35, f32[8,32]{1,0:T(8,128)S(1)} %get-tuple-element.32, f32[8,32,16]{1,2,0:T(8,128)S(1)} %fusion.37), channel_id=1, replica_groups=mesh['member'=8,'node'=64] {'node'}, use_global_device_ids=true, to_apply=%region_1.0 | all-reduce | flops 8448 | bytes 67584 | tf_op jit(solution)/shard_map/psum | solution.py:77
  573.2 1.1 fusion.22
  574.3 1.1 fusion.19
  575.3 1.1 fusion.25
  576.4 0.4 fusion.34
  576.9 0.2 convolution_convert_fusion.4
  577.1 0.3 fusion.16
  577.5 0.4 multiply_reduce_fusion.2
  577.9 0.3 fusion.29
  578.2 0.3 fusion.30
  578.5 0.4 convolution_convert_fusion.1
  579.0 0.2 copy-done.2
  579.1 0.7 fusion.36
  579.9 0.2 fusion.17
  580.0 0.2 convolution_add_fusion.4
  580.2 0.2 multiply_reduce_fusion.3
  580.4 1.1 fusion.9
  581.5 0.5 fusion.33
  582.0 1.0 copy-done.3
  583.0 1.1 convolution_bitcast_fusion.1
  584.0 0.7 fusion.4
  584.8 1.4 copy-done.11
  586.2 1.9 multiply_reduce_fusion
  588.1 1.3 copy-done.7
  589.4 0.4 convolution_convert_fusion
  589.8 1.1 convolution_bitcast_fusion.2
  590.9 0.2 convolution_bitcast_fusion.4
  591.1 0.2 convolution_bitcast_fusion.5
  591.3 2.3 convolution_bitcast_fusion.6
  593.6 1.8 fusion.38
  595.4 0.1 reduce_sum.85
  595.5 3.4 fusion.5
  598.9 112.6 %all-reduce = (f32[128]{0:T(128)}, f32[16,32]{1,0:T(8,128)}, f32[8]{0:T(128)}) all-reduce(f32[128]{0:T(128)S(1)} %reduce_sum.85, f32[16,32]{1,0:T(8,128)S(1)} %convolution_bitcast_fusion.6, f32[8]{0:T(128)S(1)} %negate_divide_fusion), channel_id=1, replica_groups=mesh['member'=8,'node'=64] {'member','node'}, use_global_device_ids=true, to_apply=%region_12.0 | all-reduce | flops 648 | bytes 5184 | tf_op jit(solution)/shard_map/psum | solution.py:158
  711.5 0.2 convolution_bitcast_fusion.3
  711.7 45.1 %all-reduce.3 = (f32[16,16]{1,0:T(8,128)}, f32[16,16]{1,0:T(8,128)}, f32[16,16]{1,0:T(8,128)}) all-reduce(f32[16,16]{1,0:T(8,128)S(1)} %convolution_bitcast_fusion.5, f32[16,16]{1,0:T(8,128)S(1)} %convolution_bitcast_fusion.4, f32[16,16]{1,0:T(8,128)S(1)} %convolution_bitcast_fusion.3), channel_id=1, replica_groups=mesh['member'=8,'node'=64] {'member'}, use_global_device_ids=true, to_apply=%region_16.0 | all-reduce | flops 768 | bytes 6144 | tf_op jit(solution)/shard_map/psum | solution.py:157
  756.8 294.2 %all-reduce.6.cloned.1.call-done = (f32[128,128]{0,1:T(8,128)}, f32[128,128]{0,1:T(8,128)}, f32[128,128]{1,0:T(8,128)}) async-done(((f32[128,128]{0,1:T(8,128)}, f32[128,128]{0,1:T(8,128)}, f32[128,128]{1,0:T(8,128)}), (f32[128,128]{0,1:T(8,128)}, f32[128,128]{0,1:T(8,128)}, f32[128,128]{1,0:T(8,128)})) %all-reduce.6.cloned.1.call-update) | async-done | bytes 196624 | tf_op jit(solution)/shard_map/psum | solution.py:158
  1050.9 1.6 copy.28
  1052.5 1.6 copy.29
  1054.1 1.5 copy.43
  (53 shorter events, 0.2 us)
Async XLA Ops:
  7.2 1.2 copy-start
  7.2 2.5 copy-start.15
  7.2 2.5 copy-start.24
  7.2 3.0 copy-start.12
  7.2 3.0 copy-start.19
  7.2 1043.7 %all-reduce.6.cloned.1.call-start = ((), (), s32[]{:S(2)}) async-start(), calls=%async_computation | async-start | bytes 393216 | tf_op jit(solution)/shard_map/psum | solution.py:158
  9.7 1.0 copy-start.8
  9.7 1.0 copy-start.21
  9.7 1.0 copy-start.25
  10.2 4.2 copy-start.5
  10.7 3.1 copy-start.1
  11.8 1.9 copy-start.10
  14.4 558.8 %copy-start.23 = (bf16[16,16]{1,0:T(8,128)(2,1)S(1)}, bf16[16,16]{1,0:T(8,128)(2,1)}, u32[]{:S(2)}) copy-start(bf16[16,16]{1,0:T(8,128)(2,1)} %param.19) | copy-start | bytes 1540
  14.4 559.8 %copy-start.22 = (bf16[16,16]{1,0:T(8,128)(2,1)S(1)}, bf16[16,16]{1,0:T(8,128)(2,1)}, u32[]{:S(2)}) copy-start(bf16[16,16]{1,0:T(8,128)(2,1)} %param.20) | copy-start | bytes 1540
  14.4 560.9 %copy-start.20 = (bf16[16,16]{1,0:T(8,128)(2,1)S(1)}, bf16[16,16]{1,0:T(8,128)(2,1)}, u32[]{:S(2)}) copy-start(bf16[16,16]{1,0:T(8,128)(2,1)} %param.18) | copy-start | bytes 1540
  577.4 2.4 copy-start.16
  577.9 1.2 copy-start.2
  579.1 1.1 copy-start.18
  579.1 1.3 copy-start.13
  581.5 2.6 copy-start.6
  582.0 1.0 copy-start.3
  584.0 2.2 copy-start.11
  588.1 1.3 copy-start.7
  589.8 1.5 copy-start.9
  590.9 2.7 copy-start.14
  593.6 1.9 copy-start.4
  595.5 116.0 %copy-start.17 = (f32[8,32,16]{1,2,0:T(8,128)S(1)}, f32[8,32,16]{1,2,0:T(8,128)}, u32[]{:S(2)}) copy-start(f32[8,32,16]{1,2,0:T(8,128)} %copy-done.16) | copy-start | bytes 49156
Sparse Core Ops, SparseCore 0:
  591.0 459.8 all-reduce.5
where the time goes:
time: 1060 us
  blocking collectives  716 us (68%)
  waiting for transfers between devices  294 us (28%)
  matrix products  24.3 us (2%)
  between operations  14.5 us (1%)
  local copies, waits for them, and re-layouts  10.8 us (1%)
    psum x1, blocking collectives, shards(): lax.psum((pooled_numerator, denominator), 'node')  558 us
    psum x1, waiting for transfers between devices, shards(): lax.psum(dominant_summands + trailing_summands, ('member', 'node'))  294 us
    psum x1, blocking collectives, shards(): lax.psum(dominant_summands + trailing_summands, ('member', 'node'))  113 us
    psum x1, blocking collectives, shards(): lax.psum((token_terms[0], token_terms[1], token_terms[2]), 'member')  45.1 us
  transfers between devices with their start and end apart: 1, of which 1 were waited for; matrix products, arithmetic and copies ran while one was open for 1% of the time, Pallas kernels for 0%

commit v1 on v0

--- a/solution.py
+++ b/solution.py
@@ -3,7 +3,7 @@
 import jax
 import jax.numpy as jnp
 from jax import lax
-from jax.sharding import PartitionSpec as P
+from jax.sharding import Mesh, PartitionSpec as P
 
 MODEL_WIDTH = 128
 NUM_CHANNELS = 8
@@ -11,6 +11,49 @@
 
 
 epsilon = 1e-05
+
+NODE = ("y", "zh", "x", "core")
+PLANE = ("y", "x", "core")
+COLUMN = ("zl", "zh")
+TOKEN_ROWS = 66
+GRAD_ROWS = 416
+
+
+def exchange(block, axes, copies):
+    sent = jnp.broadcast_to(block[None], (copies,) + block.shape)
+    return lax.all_to_all(sent, axes, 0, 0, tiled=True)
+
+
+def sum_over_nodes(rows):
+    half = TOKEN_ROWS // 2
+    halves = rows.reshape(1, 2, half, 128)
+    sent = jnp.broadcast_to(halves, (2, 2, half, 128)).reshape(4, half, 128)
+    part = jnp.sum(lax.all_to_all(sent, ("zh", "core"), 0, 0, tiled=True), 0)
+    part = jnp.sum(exchange(part, ("y", "x"), 16), 0)
+    return lax.all_gather(part, "core", axis=0, tiled=True)
+
+
+def sum_over_all(rows):
+    parts = lax.all_to_all(rows.reshape(32, GRAD_ROWS // 32, 128), PLANE, 0, 0, tiled=True)
+    part = jnp.sum(parts, 0)
+    part = jnp.sum(exchange(part, COLUMN, 16), 0)
+    return exchange(part, PLANE, 32).reshape(GRAD_ROWS, 128)
+
+
+def pack(arrays, rows):
+    flat = jnp.concatenate([a.reshape(-1) for a in arrays])
+    return jnp.pad(flat, (0, rows * 128 - flat.shape[0])).reshape(rows, 128)
+
+
+def unpack(rows, shapes):
+    flat = rows.reshape(-1)
+    out = []
+    at = 0
+    for shape in shapes:
+        size = math.prod(shape)
+        out.append(flat[at : at + size].reshape(shape))
+        at += size
+    return out
 
 
 def attend(physical_state_vectors, state_asking_map, state_lookup_map, state_content_map):
@@ -74,7 +117,18 @@
         "wou,wog->oug", probability_halfway, feature_halfway, preferred_element_type=jnp.float32
     )
     denominator = jnp.sum(probs, 0)
-    pooled_numerator, denominator = lax.psum((pooled_numerator, denominator), "node")
+    backward_halfway = (
+        jnp.dot(incoming_sensitivity, result_projection.T, preferred_element_type=jnp.float32)
+        .astype(jnp.bfloat16)
+        .reshape(mesh_node_rows, NUM_CHANNELS, D)
+    )
+    slice_token_gradient = jnp.einsum(
+        "wou,wog->oug", probability_halfway, backward_halfway, preferred_element_type=jnp.float32
+    )
+    pooled = (pooled_numerator, slice_token_gradient, denominator)
+    pooled_numerator, slice_token_gradient, denominator = unpack(
+        sum_over_nodes(pack(pooled, TOKEN_ROWS)), [a.shape for a in pooled]
+    )
     physical_state_vectors = pooled_numerator / (denominator[:, :, None] + epsilon)
     token_out, attend_back = jax.vjp(
         attend,
@@ -91,18 +145,9 @@
         .reshape(mesh_node_rows, MODEL_WIDTH)
         .astype(jnp.bfloat16)
     )
-    backward_halfway = (
-        jnp.dot(incoming_sensitivity, result_projection.T, preferred_element_type=jnp.float32)
-        .astype(jnp.bfloat16)
-        .reshape(mesh_node_rows, NUM_CHANNELS, D)
-    )
     mapping_contribution = jnp.dot(
         mixed_half.T, incoming_sensitivity, preferred_element_type=jnp.float32
     )
-    slice_token_gradient = jnp.einsum(
-        "wou,wog->oug", probability_halfway, backward_halfway, preferred_element_type=jnp.float32
-    )
-    slice_token_gradient = lax.psum(slice_token_gradient, "node")
     piece_reverse_derivative, asking_contribution, lookup_contribution, content_contribution = (
         attend_back(slice_token_gradient)
     )
@@ -153,11 +198,15 @@
     ) + jnp.dot(feat_back_half, aggregate_projection.T, preferred_element_type=jnp.float32)
     dominant_summands = (hidden_contribution, channel_contribution, mapping_contribution)
     trailing_summands = (shift_term_derivative, division_term_derivative, inverse_spread_derivative)
-    token_terms = (asking_contribution, lookup_contribution, content_contribution)
-    piece_totals = lax.psum((token_terms[0], token_terms[1], token_terms[2]), "member")
-    totalled = lax.psum(dominant_summands + trailing_summands, ("member", "node"))
+    token_terms = tuple(
+        term * (1.0 / 64.0)
+        for term in (asking_contribution, lookup_contribution, content_contribution)
+    )
+    terms = dominant_summands + trailing_summands + token_terms
+    totalled = unpack(sum_over_all(pack(terms, GRAD_ROWS)), [a.shape for a in terms])
     large_sums = totalled[:3]
-    small_sums = totalled[3:]
+    small_sums = totalled[3:6]
+    piece_totals = totalled[6:]
     return (
         vertex_sensitivity[None],
         large_sums[0],
@@ -173,9 +222,10 @@
 
 
 def solution(mesh):
+    fine = Mesh(mesh.devices.reshape(8, 4, 2, 4, 2), ("zl",) + NODE)
     placed = (
-        P("member", "node", None),
-        P("member", "node", None),
+        P("zl", NODE, None),
+        P("zl", NODE, None),
         P(),
         P(),
         P(),
@@ -188,8 +238,8 @@
     )
     return jax.shard_map(
         shards,
-        mesh=mesh,
+        mesh=fine,
         in_specs=placed,
-        out_specs=(P("member", "node", None), P(), P(), P(), P(), P(), P(), P(), P(), P()),
+        out_specs=(P("zl", NODE, None), P(), P(), P(), P(), P(), P(), P(), P(), P()),
         check_vma=False,
     )

time: 1060 us -> 137 us (0.13)
  blocking collectives: 716 us -> 59.6 us
  waiting for transfers between devices: 294 us -> 17.2 us
  between operations: 14.5 us -> 1.18 us
  starting transfers between devices: 0.04 us -> 11.1 us
    psum x3 -> x0, blocking collectives: 716 us -> none  [the longest x1 558 us: shards(): lax.psum((pooled_numerator, denominator), 'node')]
    psum x1 -> x0, waiting for transfers between devices: 294 us -> none  [shards(): lax.psum(dominant_summands + trailing_summands, ('member', 'node'))]
    all_to_all x0 -> x3, blocking collectives: none -> 55.7 us  [the longest x1 28.4 us: sum_over_nodes(): part = jnp.sum(lax.all_to_all(sent, ('zh', 'core'), 0, 0, tiled=True), 0)]
    all_to_all x0 -> x2, waiting for transfers between devices: none -> 17.2 us  [exchange(): return lax.all_to_all(sent, axes, 0, 0, tiled=True)]
    all_to_all x0 -> x2, starting transfers between devices: none -> 11.1 us  [exchange(): return lax.all_to_all(sent, axes, 0, 0, tiled=True)]
  transfers between devices with their start and end apart: 1 -> 2, of which waited for: 1 -> 2; matrix products, arithmetic and copies ran while one was open for 1% -> 4% of each run, Pallas kernels for 0% -> 0%
where the time goes in v1:
time: 137 us; the launch traced here: 136 us
  blocking collectives  59.6 us (44%)
  matrix products  23.3 us (17%)
  local copies, waits for them, and re-layouts  19.2 us (14%)
  waiting for transfers between devices  17.2 us (13%)
  starting transfers between devices  11.1 us (8%)
  other arithmetic  4.42 us (3%)
    all_to_all x1, blocking collectives, sum_over_nodes(): part = jnp.sum(lax.all_to_all(sent, ('zh', 'core'), 0, 0, tiled=True), 0)  28.4 us
    all_to_all x2, waiting for transfers between devices, exchange(): return lax.all_to_all(sent, axes, 0, 0, tiled=True)  17.2 us
    all_to_all x1, blocking collectives, exchange(): return lax.all_to_all(sent, axes, 0, 0, tiled=True)  14.7 us
    all_to_all x1, blocking collectives, sum_over_all(): lax.all_to_all(rows.reshape(32, GRAD_ROWS // 32, 128), PLANE, 0, 0, tiled...  12.7 us
    all_to_all x2, starting transfers between devices, exchange(): return lax.all_to_all(sent, axes, 0, 0, tiled=True)  11.1 us
    unnamed x45, local copies, waits for them, and re-layouts  5.6 us
    all_gather x1, blocking collectives, sum_over_nodes(): return lax.all_gather(part, 'core', axis=0, tiled=True)  3.9 us
    dot_general x1, matrix products, shards(): jnp.dot(feat_back_half, aggregate_projection.T, preferred_element_type=jn...  3.38 us
  transfers between devices with their start and end apart: 2, of which 2 were waited for; matrix products, arithmetic and copies ran while one was open for 4% of the time, Pallas kernels for 0%

profile of v1, /device:TPU:1, one launch (start us, length us, event | category | flops | bytes accessed | tf_op | source)
XLA Modules:
  0.0 136.1 jit_solution(5086780622887115443)
XLA Ops:
  0.7 1.2 copy-done
  1.9 1.2 convolution_convert_fusion.3
  3.1 1.1 exponential_reduce_fusion
  4.3 1.0 fusion.34
  5.3 0.9 copy-done.6
  6.3 1.7 %convolution_convert_fusion.2 = bf16[4096,128]{0,1:T(8,128)(2,1)S(1)} fusion(bf16[128,128]{1,0:T(8,128)(2,1)S(1)} %copy-done.15, bf16[1,4096,128]{2,1,0:T(8,128)(2,1)} %param.12), kind=kOutput, calls=%fused_computation.13 | convolution fusion | flops 134742016 | bytes 2129920 | tf_op jit(solution)/shard_map/dot_general | solution.py:121
  8.0 0.9 copy-done.4
  9.0 0.8 fusion.41
  9.9 0.5 fusion.6
  10.4 1.0 copy-done.8
  11.4 0.8 fusion.40
  12.3 28.4 %all_to_all.25 = f32[4,33,128]{2,1,0:T(8,128)S(1)} all-to-all(f32[4,33,128]{2,1,0:T(8,128)S(1)} %bitcast.128), channel_id=1, replica_groups=mesh['zl'=8,'y'=4,'zh'=2,'x'=4,'core'=2] {'zh','core'}, dimensions={0} | all-to-all | bytes 135168 | tf_op jit(solution)/shard_map/all_to_all | solution.py:31
  40.7 14.7 %all_to_all.26 = f32[16,33,128]{2,1,0:T(8,128)S(1)} all-to-all(f32[16,33,128]{2,1,0:T(8,128)S(1)} %broadcast_in_dim.18), channel_id=1, replica_groups=mesh['zl'=8,'y'=4,'zh'=2,'x'=4,'core'=2] {'y','x'}, dimensions={0} | all-to-all | bytes 540672 | tf_op jit(solution)/shard_map/all_to_all | solution.py:24
  55.4 3.9 %all-gather = f32[2,33,128]{2,1,0:T(8,128)S(1)} all-gather(f32[1,33,128]{2,1,0:T(8,128)S(1)} %bitcast.131), channel_id=1, replica_groups=mesh['zl'=8,'y'=4,'zh'=2,'x'=4,'core'=2] {'core'}, dimensions={0}, use_global_device_ids=true | all-gather | bytes 50688 | tf_op jit(solution)/shard_map/all_gather | solution.py:33
  61.5 0.4 multiply_reduce_fusion.2
  63.0 1.4 %convolution_convert_fusion.1 = bf16[8,16,4096]{2,1,0:T(8,128)(2,1)} fusion(bf16[8,32,16]{1,2,0:T(8,128)(2,1)S(1)} %convolution_convert_fusion.4, bf16[4096,8,32]{0,2,1:T(8,128)(2,1)S(1)} %get-tuple-element.10), kind=kOutput, calls=%fused_computation.12 | convolution fusion | flops 34078720 | bytes 3153920 | tf_op jit(solution)/shard_map/afq,fqx->afx/dot_general | solution.py:142
  64.4 0.7 fusion.42
  66.0 1.4 %fusion.35 = (f32[8,16]{1,0:T(8,128)S(1)}, bf16[4096,8,16]{0,2,1:T(8,128)(2,1)}) fusion(bf16[4096,8,32]{0,2,1:T(8,128)(2,1)S(1)} %get-tuple-element.10, f32[8,32,16]{1,2,0:T(8,128)S(1)} %get-tuple-element.33, f32[8,32]{1,0:T(8,128)S(1)} %get-tuple-element.24), kind=kOutput, calls=%fused_computation.72 | convolution fusion | flops 34611072 | bytes 3163648 | tf_op jit(solution)/shard_map/afq,fqx->afx/dot_general | solution.py:164
  67.4 0.8 fusion.4
  68.1 1.4 %copy-done.7 = f32[4096,8,32]{0,2,1:T(8,128)S(1)} copy-done((f32[4096,8,32]{0,2,1:T(8,128)S(1)}, f32[4096,8,32]{0,2,1:T(8,128)}, u32[]{:S(2)}) %copy-start.7) | copy-done | bytes 4194328
  69.6 1.8 %multiply_reduce_fusion = (f32[8]{0:T(128)S(1)}, bf16[4096,8,32]{0,2,1:T(8,128)(2,1)S(1)}) fusion(f32[4096,8,32]{0,2,1:T(8,128)S(1)} %copy-done.7, f32[8]{0:T(128)S(1)} %copy-done.21, f32[4096,8,32]{0,2,1:T(8,128)S(1)} %fusion.4, f32[4096,8]{0,1:T(8,128)S(1)} %copy-done.14), kind=kOutput, calls=%fused_computation.16 | output fusion | flops 9469975 | bytes 10616896 | tf_op jit(solution)/shard_map/sub | solution.py:170
  71.4 0.7 convolution_bitcast_fusion.7
  72.1 0.4 convolution_convert_fusion
  72.6 0.6 reshape.162
  73.2 0.6 reshape.164
  73.9 0.6 reduce_sum.123
  74.5 2.0 %convolution_bitcast_fusion.1 = f32[16384]{0:T(1024)S(1)} fusion(bf16[4096,128]{0,1:T(8,128)(2,1)} %bitcast.125, bf16[1,4096,128]{2,1,0:T(8,128)(2,1)} %param.12), kind=kOutput, calls=%fused_computation.22 | convolution fusion | flops 134217728 | bytes 2162688 | tf_op jit(solution)/shard_map/dot_general | solution.py:148
  77.0 0.5 negate_divide_fusion
  78.1 3.1 %concatenate.7 = f32[50568]{0:T(1024)S(1)} concatenate(f32[16384]{0:T(1024)S(1)} %bitcast.130, f32[16384]{0:T(1024)S(1)} %bitcast.129, f32[16384]{0:T(1024)S(1)} %convolution_bitcast_fusion.1, f32[128]{0:T(128)} %reduce_sum.123, f32[512]{0:T(512)S(1)} %reshape.161, f32[8]{0:T(128)} %negate_divide_fusion, f32[256]{0:T(256)} %reshape.162, f32[256]{0:T(256)S(1)} %reshape.163, ...), dimensions={0} | concatenate | bytes 404544 | tf_op jit(solution)/shard_map/concatenate | solution.py:44
  81.2 0.7 pad.4
  81.9 1.0 reshape_reshape.7
  82.8 12.7 %all_to_all.27 = f32[32,13,128]{2,1,0:T(8,128)} all-to-all(f32[32,13,128]{2,1,0:T(8,128)S(1)} %reshape_reshape.7), channel_id=1, replica_groups=mesh['zl'=8,'y'=4,'zh'=2,'x'=4,'core'=2] {'y','x','core'}, dimensions={0} | all-to-all | bytes 425984 | tf_op jit(solution)/shard_map/all_to_all | solution.py:37
  95.5 1.0 reduce_sum.125
  96.5 0.6 broadcast_in_dim.22
  97.1 4.9 %all-to-all-start.3 = ((f32[16,13,128]{2,1,0:T(8,128)}), f32[16,13,128]{2,1,0:T(8,128)S(1)}, u32[]{:S(2)}, u32[]{:S(2)}) async-start(f32[16,13,128]{2,1,0:T(8,128)} %broadcast_in_dim.22), calls=%async_computation.3 | async-start | bytes 262144 | tf_op jit(solution)/shard_map/all_to_all | solution.py:24
  102.0 1.8 %fusion.43 = f32[4096,128]{1,0:T(8,128)} fusion(bf16[4096,128]{0,1:T(8,128)(2,1)S(1)} %bitcast.120, bf16[128,128]{1,0:T(8,128)(2,1)S(1)} %copy-done.10), kind=kOutput, calls=%fused_computation.80 | convolution fusion | flops 134217728 | bytes 3178496 | tf_op jit(solution)/shard_map/dot_general | solution.py:196
  103.8 11.6 %all-to-all-done.3 = f32[16,13,128]{2,1,0:T(8,128)S(1)} async-done(((f32[16,13,128]{2,1,0:T(8,128)}), f32[16,13,128]{2,1,0:T(8,128)S(1)}, u32[]{:S(2)}, u32[]{:S(2)}) %all-to-all-start.3) | async-done | bytes 106528 | tf_op jit(solution)/shard_map/all_to_all | solution.py:24
  115.4 0.7 broadcast_in_dim.23
  116.1 6.3 %all-to-all-start.4 = ((f32[32,13,128]{2,1,0:T(8,128)}), f32[32,13,128]{2,1,0:T(8,128)S(1)}, u32[]{:S(2)}, u32[]{:S(2)}) async-start(f32[32,13,128]{2,1,0:T(8,128)} %broadcast_in_dim.23), calls=%async_computation.4 | async-start | bytes 524288 | tf_op jit(solution)/shard_map/all_to_all | solution.py:24
  122.4 3.4 %fusion.5 = f32[1,4096,128]{2,1,0:T(8,128)} fusion(f32[4096,128]{1,0:T(8,128)} %fusion.43, bf16[4096,128]{0,1:T(8,128)(2,1)S(1)} %bitcast.118, bf16[128,128]{1,0:T(8,128)(2,1)S(1)} %copy-done.12), kind=kOutput, calls=%fused_computation.7 | convolution fusion | flops 134742016 | bytes 5275648 | tf_op jit(solution)/shard_map/dot_general | solution.py:198
  125.8 5.6 %all-to-all-done.4 = f32[32,13,128]{2,1,0:T(8,128)S(1)} async-done(((f32[32,13,128]{2,1,0:T(8,128)}), f32[32,13,128]{2,1,0:T(8,128)S(1)}, u32[]{:S(2)}, u32[]{:S(2)}) %all-to-all-start.4) | async-done | bytes 213024 | tf_op jit(solution)/shard_map/all_to_all | solution.py:24
  131.5 0.5 slice.68
  132.0 0.5 slice.66
  132.6 0.7 reshape.167
  133.2 0.7 reshape.166
  133.9 0.7 reshape.165
  134.6 0.7 fusion.36
  135.5 0.6 slice.67
  (83 shorter events, 5.9 us)
Async XLA Ops:
  0.6 1.2 copy-start
  0.7 2.5 %copy-start.21 = (f32[8]{0:T(128)S(1)}, f32[8]{0:T(128)}, u32[]{:S(2)}) copy-start(f32[8]{0:T(128)} %param.17) | copy-start | bytes 100
  0.7 2.5 %copy-start.17 = (bf16[16,32]{1,0:T(8,128)(2,1)S(1)}, bf16[16,32]{1,0:T(8,128)(2,1)}, u32[]{:S(2)}) copy-start(bf16[16,32]{1,0:T(8,128)(2,1)} %param.16) | copy-start | bytes 3076
  3.1 1.2 copy-start.2
  4.3 1.9 %copy-start.6 = (f32[4096,8,32]{0,2,1:T(8,128)}, f32[4096,8,32]{0,2,1:T(8,128)S(1)}, u32[]{:S(2)}) copy-start(f32[4096,8,32]{0,2,1:T(8,128)S(1)} %get-tuple-element.27) | copy-start | bytes 12582916
  4.3 2.0 %copy-start.13 = (f32[4096,8]{0,1:T(8,128)}, f32[4096,8]{0,1:T(8,128)S(1)}, u32[]{:S(2)}) copy-start(f32[4096,8]{0,1:T(8,128)S(1)} %get-tuple-element.26) | copy-start | bytes 393220
  4.3 2.0 %copy-start.15 = (bf16[128,128]{1,0:T(8,128)(2,1)S(1)}, bf16[128,128]{1,0:T(8,128)(2,1)}, u32[]{:S(2)}) copy-start(bf16[128,128]{1,0:T(8,128)(2,1)} %param.21) | copy-start | bytes 98308
  8.0 1.0 copy-start.4
  8.0 1.8 %copy-start.11 = (bf16[128,128]{1,0:T(8,128)(2,1)S(1)}, bf16[128,128]{1,0:T(8,128)(2,1)}, u32[]{:S(2)}) copy-start(bf16[128,128]{1,0:T(8,128)(2,1)} %param.14) | copy-start | bytes 98308
  8.0 1.8 %copy-start.20 = (f32[128]{0:T(128)S(1)}, f32[128]{0:T(128)}, u32[]{:S(2)}) copy-start(f32[128]{0:T(128)} %param.15) | copy-start | bytes 1540
  10.4 1.0 copy-start.8
  12.1 47.6 %copy-start.19 = (bf16[16,16]{1,0:T(8,128)(2,1)S(1)}, bf16[16,16]{1,0:T(8,128)(2,1)}, u32[]{:S(2)}) copy-start(bf16[16,16]{1,0:T(8,128)(2,1)} %param.19) | copy-start | bytes 1540
  12.1 47.8 %copy-start.18 = (bf16[16,16]{1,0:T(8,128)(2,1)S(1)}, bf16[16,16]{1,0:T(8,128)(2,1)}, u32[]{:S(2)}) copy-start(bf16[16,16]{1,0:T(8,128)(2,1)} %param.20) | copy-start | bytes 1540
  12.1 48.1 %copy-start.16 = (bf16[16,16]{1,0:T(8,128)(2,1)S(1)}, bf16[16,16]{1,0:T(8,128)(2,1)}, u32[]{:S(2)}) copy-start(bf16[16,16]{1,0:T(8,128)(2,1)} %param.18) | copy-start | bytes 1540
  62.2 2.2 %copy-start.5 = (bf16[4096,128]{0,1:T(8,128)(2,1)S(1)}, bf16[4096,128]{0,1:T(8,128)(2,1)}, u32[]{:S(2)}) copy-start(bf16[4096,128]{0,1:T(8,128)(2,1)} %copy-done.4) | copy-start | bytes 3145732
  65.2 2.2 %copy-start.9 = (bf16[4096,128]{0,1:T(8,128)(2,1)S(1)}, bf16[4096,128]{0,1:T(8,128)(2,1)}, u32[]{:S(2)}) copy-start(bf16[4096,128]{0,1:T(8,128)(2,1)} %copy-done.8) | copy-start | bytes 3145732
  67.4 2.2 %copy-start.7 = (f32[4096,8,32]{0,2,1:T(8,128)S(1)}, f32[4096,8,32]{0,2,1:T(8,128)}, u32[]{:S(2)}) copy-start(f32[4096,8,32]{0,2,1:T(8,128)} %copy-done.6) | copy-start | bytes 12582916
  67.4 2.2 %copy-start.14 = (f32[4096,8]{0,1:T(8,128)S(1)}, f32[4096,8]{0,1:T(8,128)}, u32[]{:S(2)}) copy-start(f32[4096,8]{0,1:T(8,128)} %copy-done.13) | copy-start | bytes 393220
  69.6 1.8 %copy-start.3 = (bf16[4096,128]{0,1:T(8,128)(2,1)S(1)}, bf16[4096,128]{0,1:T(8,128)(2,1)}, u32[]{:S(2)}) copy-start(bf16[4096,128]{0,1:T(8,128)(2,1)} %copy-done.2) | copy-start | bytes 3145732
  72.1 4.4 %copy-start.1 = (bf16[4096,8,16]{0,2,1:T(8,128)(2,1)S(1)}, bf16[4096,8,16]{0,2,1:T(8,128)(2,1)}, u32[]{:S(2)}) copy-start(bf16[4096,8,16]{0,2,1:T(8,128)(2,1)} %get-tuple-element.15) | copy-start | bytes 3145732
  81.2 20.8 %copy-start.10 = (bf16[128,128]{1,0:T(8,128)(2,1)S(1)}, bf16[128,128]{1,0:T(8,128)(2,1)}, u32[]{:S(2)}) copy-start(bf16[128,128]{1,0:T(8,128)(2,1)} %param.13) | copy-start | bytes 98308
  97.1 18.3 %all-to-all-start.3 = ((f32[16,13,128]{2,1,0:T(8,128)}), f32[16,13,128]{2,1,0:T(8,128)S(1)}, u32[]{:S(2)}, u32[]{:S(2)}) async-start(f32[16,13,128]{2,1,0:T(8,128)} %broadcast_in_dim.22), calls=%async_computation.3 | async-start | bytes 262144 | tf_op jit(solution)/shard_map/all_to_all | solution.py:24
  102.0 20.5 %copy-start.12 = (bf16[128,128]{1,0:T(8,128)(2,1)S(1)}, bf16[128,128]{1,0:T(8,128)(2,1)}, u32[]{:S(2)}) copy-start(bf16[128,128]{1,0:T(8,128)(2,1)} %param.14) | copy-start | bytes 98308
  116.1 15.3 %all-to-all-start.4 = ((f32[32,13,128]{2,1,0:T(8,128)}), f32[32,13,128]{2,1,0:T(8,128)S(1)}, u32[]{:S(2)}, u32[]{:S(2)}) async-start(f32[32,13,128]{2,1,0:T(8,128)} %broadcast_in_dim.23), calls=%async_computation.4 | async-start | bytes 524288 | tf_op jit(solution)/shard_map/all_to_all | solution.py:24

commit v2 on v0

v2 whole, which is shorter than its diff:
```python
import jax
import jax.numpy as jnp
from jax import lax
from jax.experimental import pallas as pl
from jax.experimental.pallas import tpu as pltpu
from jax.sharding import Mesh, PartitionSpec as P

HEADS = 8
SLICES = 32
D = 16
WIDTH = HEADS * D
LANES = HEADS * SLICES
EPS = 1e-05
TILE = 1024
NODE = ("y", "zh", "x", "core")
PLANE = ("y", "x", "core")
COLUMN = ("zl", "zh")
F32 = jnp.float32
BF16 = jnp.bfloat16
EXACT = lax.Precision.HIGHEST


def dot(a, b, ca=1, cb=0, precision=None):
    return lax.dot_general(
        a, b, (((ca,), (cb,)), ((), ())), precision=precision, preferred_element_type=F32
    )


def grid_of(shape):
    return lax.broadcasted_iota(jnp.int32, shape, 0), lax.broadcasted_iota(jnp.int32, shape, 1)


def match(shape, f, g):
    r, c = grid_of(shape)
    return f(r) == g(c)


def head16(i):
    return i >> 4


def head32(i):
    return i >> 5


def in16(i):
    return i & 15


def in32(i):
    return i & 31


def same(i):
    return i


def block_slices(a16x32):
    rows = dot(match((WIDTH, D), in16, same).astype(BF16), a16x32).astype(BF16)
    wide = dot(rows, match((SLICES, LANES), same, in32).astype(BF16))
    return jnp.where(match((WIDTH, LANES), head16, head32), wide, 0.0)


def block_square(a16x16):
    rows = dot(match((WIDTH, D), in16, same).astype(BF16), a16x16).astype(BF16)
    wide = dot(rows, match((D, WIDTH), same, in16).astype(BF16))
    return jnp.where(match((WIDTH, WIDTH), head16, head16), wide, 0.0)


def sharpness_row(sharp):
    col = lax.broadcasted_iota(jnp.int32, (1, LANES), 1) >> 5
    row = jnp.zeros((1, LANES), F32)
    for h in range(HEADS):
        row = jnp.where(col == h, sharp[h], row)
    return 1.0 / row


def group_sum(a, ones):
    high = a.astype(BF16)
    low = (a - high.astype(F32)).astype(BF16)
    return dot(high, ones) + dot(low, ones)


def fold_rows(a, rows):
    return jnp.sum(a.reshape(a.shape[0] // rows, rows, a.shape[1]), 0)


def stack_heads(a):
    tall = jnp.concatenate([a] * HEADS, 0)
    return jnp.where(match((LANES, WIDTH), head32, head16), tall, 0.0)


def pool_kernel(
    sharp, x, g, hidden, aggregate, offset, assign, result, probs_out, rows_out, pool_out,
    weights, assign_wide, scale, ones, pooled, mass,
):
    step = pl.program_id(0)

    @pl.when(step == 0)
    def _():
        weights[:, :WIDTH] = hidden[...]
        weights[:, WIDTH:] = aggregate[...]
        assign_wide[...] = block_slices(assign[...]).astype(BF16)
        scale[...] = sharpness_row(sharp)
        ones[...] = match((LANES, LANES), head32, head32).astype(BF16)
        pooled[...] = jnp.zeros_like(pooled)
        mass[...] = jnp.zeros_like(mass)

    both = dot(x[...], weights[...])
    mid = both[:, :WIDTH].astype(BF16)
    feat = (both[:, WIDTH:] + offset[...]).astype(BF16)
    back = dot(g[...], result[...], 1, 1).astype(BF16)
    rows_out[:, :WIDTH] = mid
    rows_out[:, WIDTH : 2 * WIDTH] = back
    rows_out[:, 2 * WIDTH :] = feat
    expon = jnp.exp(dot(mid, assign_wide[...]) * scale[...])
    probs = expon / group_sum(expon, ones[...])
    probs_out[...] = probs
    mass[...] += fold_rows(probs, 8)
    pooled[...] += dot(probs.astype(BF16), jnp.concatenate([back, feat], 1), 0, 0)

    @pl.when(step == pl.num_programs(0) - 1)
    def _():
        row, col = grid_of((LANES, LANES))
        kept = jnp.where((row >> 5) == ((col & 127) >> 4), pooled[...], 0.0)
        small = fold_rows(kept, SLICES)
        total = jnp.sum(mass[...], 0, keepdims=True)
        for z in range(2):
            pool_out[2 * z, :SLICES] = small[:, WIDTH:]
            pool_out[2 * z, SLICES:] = total[:, :WIDTH]
            pool_out[2 * z + 1, :SLICES] = small[:, :WIDTH]
            pool_out[2 * z + 1, SLICES:] = total[:, WIDTH:]


def attend_terms(pool, ask, look, content):
    numer = pool[0, :SLICES]
    token_grad = pool[1, :SLICES]
    mass = jnp.concatenate([pool[0, SLICES:], pool[1, SLICES:]], 1)
    spread = jnp.where(match((SLICES, LANES), same, in32), mass, 0.0)
    heads = match((LANES, WIDTH), head32, head16).astype(F32)
    lanes = match((LANES, LANES), head32, head32).astype(F32)
    denom = dot(spread, heads, precision=EXACT) + EPS
    inverse = 1.0 / denom
    tokens = numer / denom
    maps = [block_square(m[...]) for m in (ask, look, content)]
    q, k, v = [dot(tokens, m, precision=EXACT) for m in maps]
    keys = stack_heads(k)
    values = stack_heads(v)
    expon = jnp.exp(dot(q, keys, 1, 1, precision=EXACT) * 0.25)
    rows = expon / dot(expon, lanes, precision=EXACT)
    token_out = dot(rows, values, precision=EXACT)
    rows_back = dot(token_grad, values, 1, 1, precision=EXACT)
    centre = dot(rows_back * rows, lanes, precision=EXACT)
    scores_back = rows * (rows_back - centre) * 0.25
    q_back = dot(scores_back, keys, precision=EXACT)
    keep = match((LANES, WIDTH), head32, head16)
    k_back = fold_rows(jnp.where(keep, dot(scores_back, q, 0, 0, precision=EXACT), 0.0), SLICES)
    v_back = fold_rows(jnp.where(keep, dot(rows, token_grad, 0, 0, precision=EXACT), 0.0), SLICES)
    tok_back = sum(
        dot(b, m, 1, 1, precision=EXACT) for b, m in zip((q_back, k_back, v_back), maps)
    )
    numer_back = tok_back * inverse
    folded = dot(tok_back * tokens * inverse, heads, 1, 1, precision=EXACT)
    folded = jnp.where(match((SLICES, LANES), same, in32), folded, 0.0)
    denom_back = -jnp.sum(folded, 0, keepdims=True)
    square = match((WIDTH, WIDTH), head16, head16)
    lanes16 = match((WIDTH, WIDTH), in16, same).astype(F32)
    grads = []
    for b in (q_back, k_back, v_back):
        wide = jnp.where(square, dot(tokens, b, 0, 0, precision=EXACT), 0.0)
        grads.append(dot(fold_rows(wide, D), lanes16, precision=EXACT))
    return token_out, numer_back, denom_back, grads


def back_kernel(
    sharp, pool, hidden, aggregate, assign, ask, look, content, x, g, probs_in, rows_in,
    sense_out, grads_out,
    weights, assign_wide, scale, ones, token_wide, denom_back, small,
    sum_pair, sum_result, sum_slice, sum_bias, sum_heat,
):
    step = pl.program_id(0)

    @pl.when(step == 0)
    def _():
        weights[:, :WIDTH] = hidden[...]
        weights[:, WIDTH:] = aggregate[...]
        assign_wide[...] = block_slices(assign[...]).astype(BF16)
        scale[...] = sharpness_row(sharp)
        ones[...] = match((LANES, LANES), head32, head32).astype(BF16)
        token_out, numer_back, shift, grads = attend_terms(pool, ask, look, content)
        token_wide[:, :WIDTH] = stack_heads(token_out).astype(BF16)
        token_wide[:, WIDTH:] = stack_heads(numer_back).astype(BF16)
        denom_back[...] = shift
        small[...] = jnp.zeros_like(small)
        lane = lax.broadcasted_iota(jnp.int32, (D, WIDTH), 1)
        for i, term in enumerate(grads):
            moved = term if i == 0 else pltpu.roll(term, i * D, 1)
            part = jnp.where((lane >> 4) == i, moved, 0.0)
            small[:D, :] += part * (1.0 / 64.0)
        for ref in (sum_pair, sum_result, sum_slice, sum_bias, sum_heat):
            ref[...] = jnp.zeros_like(ref)

    mid = rows_in[:, :WIDTH]
    probs = probs_in[...]
    prob_back = dot(rows_in[:, WIDTH:], token_wide[...], 1, 1) + denom_back[...]
    inner = group_sum(probs * prob_back, ones[...])
    logit_back = probs * (prob_back - inner)
    sum_heat[...] += fold_rows(logit_back * dot(mid, assign_wide[...]), 8)
    score_back = (logit_back * scale[...]).astype(BF16)
    sum_slice[...] += dot(mid, score_back, 0, 0)
    mid_back = dot(score_back, assign_wide[...], 1, 1).astype(BF16)
    spread = dot(probs.astype(BF16), token_wide[...])
    mixed = spread[:, :WIDTH].astype(BF16)
    feat_wide = spread[:, WIDTH:]
    sum_bias[...] += fold_rows(feat_wide, 8)
    pair = jnp.concatenate([mid_back, feat_wide.astype(BF16)], 1)
    sum_result[...] += dot(mixed, g[...], 0, 0)
    sum_pair[...] += dot(x[...], pair, 0, 0)
    sense_out[...] = dot(pair, weights[...], 1, 1)

    @pl.when(step == pl.num_programs(0) - 1)
    def _():
        kept = jnp.where(match((WIDTH, LANES), head16, head32), sum_slice[...], 0.0)
        onto = (in32(grid_of((LANES, WIDTH))[0]) + 64) == grid_of((LANES, WIDTH))[1]
        small[:D, :] += dot(fold_rows(kept, D), onto.astype(F32), precision=EXACT)
        small[D : D + 1, :] = jnp.sum(sum_bias[...], 0, keepdims=True)
        heat = jnp.sum(sum_heat[...], 0, keepdims=True) * scale[...] * scale[...]
        heads = match((LANES, WIDTH), head32, same).astype(F32)
        heat = dot(jnp.broadcast_to(heat, (8, LANES)), heads, precision=EXACT)
        small[D + 1 : D + 2, :] = -heat[:1]
        for k in range(32):
            grads_out[k, 0:4, :] = sum_pair[4 * k : 4 * k + 4, :WIDTH]
            grads_out[k, 4:8, :] = sum_pair[4 * k : 4 * k + 4, WIDTH:]
            grads_out[k, 8:12, :] = sum_result[4 * k : 4 * k + 4, :]
            grads_out[k, 12:13, :] = small[k : k + 1, :]


def split_kernel(
    grads, mid_out, feat_out, bias_out, slice_out, heat_out, ask_out, look_out, content_out,
    result_out, small,
):
    for k in range(32):
        mid_out[4 * k : 4 * k + 4, :] = grads[k, 0:4, :]
        feat_out[4 * k : 4 * k + 4, :] = grads[k, 4:8, :]
        result_out[4 * k : 4 * k + 4, :] = grads[k, 8:12, :]
        small[k : k + 1, :] = grads[k, 12:13, :]
    ask_out[...] = small[:D, 0:D]
    look_out[...] = small[:D, D : 2 * D]
    content_out[...] = small[:D, 2 * D : 3 * D]
    slice_out[...] = small[:D, 64 : 64 + SLICES]
    bias_out[...] = small[D : D + 1, :]
    heat_out[...] = small[D + 1 : D + 2, :HEADS]


def exchange(block, axes, copies):
    sent = jnp.broadcast_to(block[None], (copies,) + block.shape)
    return lax.all_to_all(sent, axes, 0, 0, tiled=True)


def sum_over_nodes(sent):
    part = jnp.sum(lax.all_to_all(sent, ("zh", "core"), 0, 0, tiled=True), 0)
    part = jnp.sum(exchange(part, ("y", "x"), 16), 0)
    return lax.all_gather(part, "core", axis=0, tiled=False)


def sum_over_all(sent):
    part = jnp.sum(lax.all_to_all(sent, PLANE, 0, 0, tiled=True), 0)
    part = jnp.sum(exchange(part, COLUMN, 16), 0)
    return exchange(part, PLANE, 32)


def whole(shape):
    return pl.BlockSpec(shape, lambda i: (0,) * len(shape))


def tiled(width):
    return pl.BlockSpec((TILE, width), lambda i: (i, 0))


def shape(dims, dtype=F32):
    return jax.ShapeDtypeStruct(dims, dtype)


def pool(x, g, hidden, aggregate, offset, assign, sharp, result):
    nodes = x.shape[0]
    return pl.pallas_call(
        pool_kernel,
        grid=(nodes // TILE,),
        in_specs=[
            pl.BlockSpec(memory_space=pltpu.SMEM),
            tiled(WIDTH), tiled(WIDTH), whole((WIDTH, WIDTH)), whole((WIDTH, WIDTH)),
            whole((1, WIDTH)), whole((D, SLICES)), whole((WIDTH, WIDTH)),
        ],
        out_specs=[tiled(LANES), tiled(3 * WIDTH), whole((4, SLICES + 1, 128))],
        out_shape=[
            shape((nodes, LANES)), shape((nodes, 3 * WIDTH), BF16), shape((4, SLICES + 1, 128)),
        ],
        scratch_shapes=[
            pltpu.VMEM((WIDTH, LANES), BF16), pltpu.VMEM((WIDTH, LANES), BF16),
            pltpu.VMEM((1, LANES), F32), pltpu.VMEM((LANES, LANES), BF16),
            pltpu.VMEM((LANES, LANES), F32), pltpu.VMEM((8, LANES), F32),
        ],
        compiler_params=pltpu.CompilerParams(vmem_limit_bytes=48 << 20),
        name="pool",
    )(sharp, x, g, hidden, aggregate, offset, assign, result)


def back(pool_sum, x, g, hidden, aggregate, assign, sharp, ask, look, content, probs, rows):
    nodes = x.shape[0]
    return pl.pallas_call(
        back_kernel,
        grid=(nodes // TILE,),
        in_specs=[
            pl.BlockSpec(memory_space=pltpu.SMEM), whole((2, SLICES + 1, 128)),
            whole((WIDTH, WIDTH)), whole((WIDTH, WIDTH)), whole((D, SLICES)),
            whole((D, D)), whole((D, D)), whole((D, D)),
            tiled(WIDTH), tiled(WIDTH), tiled(LANES), tiled(3 * WIDTH),
        ],
        out_specs=[tiled(WIDTH), whole((32, 13, 128))],
        out_shape=[shape((nodes, WIDTH)), shape((32, 13, 128))],
        scratch_shapes=[
            pltpu.VMEM((WIDTH, LANES), BF16), pltpu.VMEM((WIDTH, LANES), BF16),
            pltpu.VMEM((1, LANES), F32), pltpu.VMEM((LANES, LANES), BF16),
            pltpu.VMEM((LANES, LANES), BF16), pltpu.VMEM((1, LANES), F32),
            pltpu.VMEM((32, 128), F32), pltpu.VMEM((WIDTH, LANES), F32),
            pltpu.VMEM((WIDTH, WIDTH), F32), pltpu.VMEM((WIDTH, LANES), F32),
            pltpu.VMEM((8, WIDTH), F32), pltpu.VMEM((8, LANES), F32),
        ],
        compiler_params=pltpu.CompilerParams(vmem_limit_bytes=48 << 20),
        name="back",
    )(sharp, pool_sum, hidden, aggregate, assign, ask, look, content, x, g, probs, rows)


def split(grads):
    square = (WIDTH, WIDTH)
    outs = [
        square, square, (1, WIDTH), (D, SLICES), (1, HEADS), (D, D), (D, D), (D, D), square,
    ]
    return pl.pallas_call(
        split_kernel,
        out_shape=[shape(s) for s in outs],
        scratch_shapes=[pltpu.VMEM((32, 128), F32)],
        name="split",
    )(grads)


def shards(
    vertex_embedding_array,
    result_sensitivity,
    hidden_projection,
    aggregate_projection,
    aggregate_offset,
    assignment_projection,
    softmax_sharpness,
    state_asking_map,
    state_lookup_map,
    state_content_map,
    result_projection,
):
    x = vertex_embedding_array[0]
    g = result_sensitivity[0]
    probs, rows, pooled = pool(
        x, g, hidden_projection, aggregate_projection, aggregate_offset[None],
        assignment_projection, softmax_sharpness, result_projection,
    )
    pool_sum = sum_over_nodes(pooled)
    sense, grads = back(
        pool_sum, x, g, hidden_projection, aggregate_projection, assignment_projection,
        softmax_sharpness, state_asking_map, state_lookup_map, state_content_map, probs, rows,
    )
    mid, feat, bias, slices, heat, ask, look, content, result = split(sum_over_all(grads))
    return sense[None], mid, feat, bias[0], slices, heat[0], ask, look, content, result


def solution(mesh):
    fine = Mesh(mesh.devices.reshape(8, 4, 2, 4, 2), ("zl",) + NODE)
    nodes = P("zl", NODE, None)
    return jax.shard_map(
        shards,
        mesh=fine,
        in_specs=(nodes, nodes) + (P(),) * 9,
        out_specs=(nodes,) + (P(),) * 9,
        check_vma=False,
    )
```

time: 1060 us -> 127 us (0.12)
  blocking collectives: 716 us -> 92.1 us
  waiting for transfers between devices: 294 us -> 0 us
  matrix products: 24.3 us -> 0 us
  Pallas kernels: 0 us -> 22.7 us
  between operations: 14.5 us -> 0.78 us
    psum x3 -> x0, blocking collectives: 716 us -> none  [the longest x1 558 us: shards(): lax.psum((pooled_numerator, denominator), 'node')]
    psum x1 -> x0, waiting for transfers between devices: 294 us -> none  [shards(): lax.psum(dominant_summands + trailing_summands, ('member', 'node'))]
    all_to_all x0 -> x5, blocking collectives: none -> 88.4 us  [the longest x3 47.9 us: exchange(): return lax.all_to_all(sent, axes, 0, 0, tiled=True)]
    dot_general x32 -> x0, matrix products: 24.3 us -> none  [the longest x1 3.41 us: shards(): jnp.dot(feat_back_half, aggregate_projection.T, preferred_element_type=jn...]
    pallas_call x0 -> x3, Pallas kernels: none -> 22.7 us  [the longest x1 14 us: back(): pl.pallas_call(back_kernel, grid=(nodes // TILE,), in_specs=[pl.BlockSpec...]
  transfers between devices with their start and end apart: 1 -> 0, of which waited for: 1 -> 0; matrix products, arithmetic and copies ran while one was open for 1% -> 0% of each run, Pallas kernels for 0% -> 0%
where the time goes in v2:
time: 127 us; the launch traced here: 126 us
  blocking collectives  92.1 us (73%)
  Pallas kernels  22.7 us (18%)
  local copies, waits for them, and re-layouts  10.4 us (8%)
    all_to_all x3, blocking collectives, exchange(): return lax.all_to_all(sent, axes, 0, 0, tiled=True)  47.9 us
    all_to_all x1, blocking collectives, sum_over_nodes(): part = jnp.sum(lax.all_to_all(sent, ('zh', 'core'), 0, 0, tiled=True), 0)  28.4 us
    pallas_call x1, Pallas kernels, back(): pl.pallas_call(back_kernel, grid=(nodes // TILE,), in_specs=[pl.BlockSpec...  14 us
    all_to_all x1, blocking collectives, sum_over_all(): part = jnp.sum(lax.all_to_all(sent, PLANE, 0, 0, tiled=True), 0)  12.1 us
    unnamed x38, local copies, waits for them, and re-layouts  10.3 us
    pallas_call x1, Pallas kernels, pool(): pl.pallas_call(pool_kernel, grid=(nodes // TILE,), in_specs=[pl.BlockSpec...  7.05 us
    all_gather x1, blocking collectives, sum_over_nodes(): return lax.all_gather(part, 'core', axis=0, tiled=False)  3.72 us

profile of v2, /device:TPU:1, one launch (start us, length us, event | category | flops | bytes accessed | tf_op | source)
XLA Modules:
  0.0 126.0 jit_solution(5266423755059310)
XLA Ops:
  0.6 0.0 copy-start.17
  0.7 0.0 copy-start.12
  0.7 0.0 copy-start
  0.7 1.2 copy-done
  1.9 0.0 copy-start.2
  1.9 1.2 copy-done.2
  3.1 0.0 copy-start.6
  3.1 0.8 copy-done.6
  3.9 0.0 copy-start.8
  3.9 0.8 copy-done.8
  4.6 0.0 copy-start.10
  4.6 0.8 copy-done.10
  5.4 0.0 copy-start.11
  5.4 0.7 copy-done.11
  6.1 0.0 copy-start.16
  6.1 0.7 copy-done.16
  6.7 0.0 copy-start.18
  6.8 0.7 copy-done.18
  7.4 0.0 copy-start.1
  7.4 0.0 copy-start.3
  7.4 0.0 copy-start.7
  7.4 0.0 copy-start.9
  7.4 0.0 copy-start.13
  7.4 0.0 copy-start.14
  7.4 0.0 copy-start.15
  7.4 7.0 %pool.1 = (f32[4096,256]{1,0:T(8,128)}, bf16[4096,384]{1,0:T(8,128)(2,1)S(1)}, f32[4,33,128]{2,1,0:T(8,128)S(1)}) custom-call(f32[8]{0:T(128)S(1)} %copy-done.16, bf16[4096,128]{1,0:T(8,128)(2,1)S(1)} %bitcast.7, bf16[4096,128]{1,0:T(8,128)(2,1)S(1)} %bitcast.9, bf16[128,128]{1,0:T(8,128)(2,1)S(1)} %copy-done.6, bf16[128,128]{1,0:T(8,128)(2,1)S(1)} %copy-done.8, ...), custom_call_target="tpu_custom_call" | custom-call | tf_op jit(solution)/shard_map/pool/pallas_call | solution.py:286
  14.5 0.0 copy-start.4
  14.5 1.7 %copy-done.4 = bf16[4096,384]{1,0:T(8,128)(2,1)} copy-done((bf16[4096,384]{1,0:T(8,128)(2,1)}, bf16[4096,384]{1,0:T(8,128)(2,1)S(1)}, u32[]{:S(2)}) %copy-start.4) | copy-done | bytes 3145752
  16.1 28.4 %all_to_all.25 = f32[4,33,128]{2,1,0:T(8,128)S(1)} all-to-all(f32[4,33,128]{2,1,0:T(8,128)S(1)} %get-tuple-element.24), channel_id=1, replica_groups=mesh['zl'=8,'y'=4,'zh'=2,'x'=4,'core'=2] {'zh','core'}, dimensions={0} | all-to-all | bytes 135168 | tf_op jit(solution)/shard_map/all_to_all | solution.py:261
  44.6 14.7 %all_to_all.26 = f32[16,33,128]{2,1,0:T(8,128)S(1)} all-to-all(f32[16,33,128]{2,1,0:T(8,128)S(1)} %broadcast_in_dim.11), channel_id=1, replica_groups=mesh['zl'=8,'y'=4,'zh'=2,'x'=4,'core'=2] {'y','x'}, dimensions={0} | all-to-all | bytes 540672 | tf_op jit(solution)/shard_map/all_to_all | solution.py:257
  59.3 3.7 %all-gather.1.pool = f32[2,33,128]{2,1,0:T(8,128)S(1)} all-gather(f32[1,33,128]{2,1,0:T(8,128)S(1)} %bitcast.12), channel_id=2, replica_groups=mesh['zl'=8,'y'=4,'zh'=2,'x'=4,'core'=2] {'core'}, dimensions={0}, use_global_device_ids=true | all-gather | bytes 50688 | tf_op jit(solution)/shard_map/all_gather | solution.py:263
  63.0 0.0 copy-done.17
  63.0 0.0 copy-done.12
  63.0 0.0 copy-done.1
  63.0 0.0 copy-done.3
  63.0 0.0 copy-done.7
  63.0 0.0 copy-done.9
  63.0 0.0 copy-done.13
  63.0 0.0 copy-done.14
  63.1 0.0 copy-done.15
  63.1 0.0 copy-start.5
  63.1 1.9 %copy-done.5 = bf16[4096,384]{1,0:T(8,128)(2,1)S(1)} copy-done((bf16[4096,384]{1,0:T(8,128)(2,1)S(1)}, bf16[4096,384]{1,0:T(8,128)(2,1)}, u32[]{:S(2)}) %copy-start.5) | copy-done | bytes 3145752
  65.0 14.0 %back.1 = (f32[4096,128]{1,0:T(8,128)}, f32[32,13,128]{2,1,0:T(8,128)S(1)}) custom-call(f32[8]{0:T(128)S(1)} %copy-done.17, f32[2,33,128]{2,1,0:T(8,128)S(1)} %all-gather.1.pool, bf16[128,128]{1,0:T(8,128)(2,1)S(1)} %copy-done.7, bf16[128,128]{1,0:T(8,128)(2,1)S(1)} %copy-done.9, bf16[16,32]{1,0:T(8,128)(2,1)S(1)} %copy-done.12, ...), custom_call_target="tpu_custom_call" | custom-call | tf_op jit(solution)/shard_map/back/pallas_call | solution.py:310
  78.9 12.1 %all_to_all.27 = f32[32,13,128]{2,1,0:T(8,128)S(1)} all-to-all(f32[32,13,128]{2,1,0:T(8,128)S(1)} %get-tuple-element.28), channel_id=1, replica_groups=mesh['zl'=8,'y'=4,'zh'=2,'x'=4,'core'=2] {'y','x','core'}, dimensions={0} | all-to-all | bytes 425984 | tf_op jit(solution)/shard_map/all_to_all | solution.py:267
  91.1 18.1 %all_to_all.28 = f32[16,13,128]{2,1,0:T(8,128)S(1)} all-to-all(f32[16,13,128]{2,1,0:T(8,128)S(1)} %broadcast_in_dim.13), channel_id=1, replica_groups=mesh['zl'=8,'y'=4,'zh'=2,'x'=4,'core'=2] {'zl','zh'}, dimensions={0} | all-to-all | bytes 212992 | tf_op jit(solution)/shard_map/all_to_all | solution.py:257
  109.3 15.1 %all_to_all.29.grads = f32[32,13,128]{2,1,0:T(8,128)} all-to-all(f32[32,13,128]{2,1,0:T(8,128)S(1)} %broadcast_in_dim.28), channel_id=1, replica_groups=mesh['zl'=8,'y'=4,'zh'=2,'x'=4,'core'=2] {'y','x','core'}, dimensions={0} | all-to-all | bytes 425984 | tf_op jit(solution)/shard_map/all_to_all | solution.py:257
  124.4 1.7 %split.1 = (f32[128,128]{1,0:T(8,128)}, f32[128,128]{1,0:T(8,128)}, f32[1,128]{1,0:T(1,128)}, f32[16,32]{1,0:T(8,128)}, f32[1,8]{1,0:T(1,128)}, /*index=5*/f32[1...) custom-call(f32[32,13,128]{2,1,0:T(8,128)} %all_to_all.29.grads), custom_call_target="tpu_custom_call" | custom-call | tf_op jit(solution)/shard_map/split/pallas_call | solution.py:339
  (7 shorter events, 0.2 us)
Async XLA Ops:
  0.6 62.4 %copy-start.17 = (f32[8]{0:T(128)S(1)}, f32[8]{0:T(128)}, u32[]{:S(2)}) copy-start(f32[8]{0:T(128)} %sharp.3) | copy-start | bytes 100
  0.7 62.3 %copy-start.12 = (bf16[16,32]{1,0:T(8,128)(2,1)S(1)}, bf16[16,32]{1,0:T(8,128)(2,1)}, u32[]{:S(2)}) copy-start(bf16[16,32]{1,0:T(8,128)(2,1)} %assign.3) | copy-start | bytes 3076
  0.7 1.2 copy-start
  1.9 1.2 copy-start.2
  3.1 0.8 copy-start.6
  3.9 0.8 copy-start.8
  4.6 0.8 copy-start.10
  5.4 0.7 copy-start.11
  6.1 0.7 copy-start.16
  6.7 0.7 copy-start.18
  7.4 55.6 %copy-start.1 = (bf16[1,4096,128]{2,1,0:T(8,128)(2,1)S(1)}, bf16[1,4096,128]{2,1,0:T(8,128)(2,1)}, u32[]{:S(2)}) copy-start(bf16[1,4096,128]{2,1,0:T(8,128)(2,1)} %param.11) | copy-start | bytes 3145732
  7.4 55.6 %copy-start.3 = (bf16[1,4096,128]{2,1,0:T(8,128)(2,1)S(1)}, bf16[1,4096,128]{2,1,0:T(8,128)(2,1)}, u32[]{:S(2)}) copy-start(bf16[1,4096,128]{2,1,0:T(8,128)(2,1)} %param.12) | copy-start | bytes 3145732
  7.4 55.6 %copy-start.7 = (bf16[128,128]{1,0:T(8,128)(2,1)S(1)}, bf16[128,128]{1,0:T(8,128)(2,1)}, u32[]{:S(2)}) copy-start(bf16[128,128]{1,0:T(8,128)(2,1)} %hidden.3) | copy-start | bytes 98308
  7.4 55.6 %copy-start.9 = (bf16[128,128]{1,0:T(8,128)(2,1)S(1)}, bf16[128,128]{1,0:T(8,128)(2,1)}, u32[]{:S(2)}) copy-start(bf16[128,128]{1,0:T(8,128)(2,1)} %aggregate.3) | copy-start | bytes 98308
  7.4 55.6 %copy-start.13 = (bf16[16,16]{1,0:T(8,128)(2,1)S(1)}, bf16[16,16]{1,0:T(8,128)(2,1)}, u32[]{:S(2)}) copy-start(bf16[16,16]{1,0:T(8,128)(2,1)} %ask.1) | copy-start | bytes 1540
  7.4 55.6 %copy-start.14 = (bf16[16,16]{1,0:T(8,128)(2,1)S(1)}, bf16[16,16]{1,0:T(8,128)(2,1)}, u32[]{:S(2)}) copy-start(bf16[16,16]{1,0:T(8,128)(2,1)} %look.1) | copy-start | bytes 1540
  7.4 55.6 %copy-start.15 = (bf16[16,16]{1,0:T(8,128)(2,1)S(1)}, bf16[16,16]{1,0:T(8,128)(2,1)}, u32[]{:S(2)}) copy-start(bf16[16,16]{1,0:T(8,128)(2,1)} %content.1) | copy-start | bytes 1540
  14.5 1.7 %copy-start.4 = (bf16[4096,384]{1,0:T(8,128)(2,1)}, bf16[4096,384]{1,0:T(8,128)(2,1)S(1)}, u32[]{:S(2)}) copy-start(bf16[4096,384]{1,0:T(8,128)(2,1)S(1)} %get-tuple-element.26.rows_in) | copy-start | bytes 9437188
  63.1 1.9 %copy-start.5 = (bf16[4096,384]{1,0:T(8,128)(2,1)S(1)}, bf16[4096,384]{1,0:T(8,128)(2,1)}, u32[]{:S(2)}) copy-start(bf16[4096,384]{1,0:T(8,128)(2,1)} %copy-done.4) | copy-start | bytes 9437188

commit v3 on v2

v3 whole, which is shorter than its diff:
```python
import jax
import jax.numpy as jnp
from jax import lax
from jax.experimental import pallas as pl
from jax.experimental.pallas import tpu as pltpu
from jax.sharding import Mesh, PartitionSpec as P

HEADS = 8
SLICES = 32
D = 16
WIDTH = HEADS * D
LANES = HEADS * SLICES
EPS = 1e-05
TILE = 2048
MEMBER = ("z4", "z2", "z1")
NODE = ("y", "zh", "x", "core")
BLOCK = ("z1", "y", "x", "core")
COLUMN = ("z4", "z2", "zh")
F32 = jnp.float32
BF16 = jnp.bfloat16


def dot(a, b, ca=1, cb=0):
    return lax.dot_general(
        a, b, (((ca,), (cb,)), ((), ())), preferred_element_type=F32
    )


def grid_of(shape):
    return lax.broadcasted_iota(jnp.int32, shape, 0), lax.broadcasted_iota(jnp.int32, shape, 1)


def match(shape, f, g):
    r, c = grid_of(shape)
    return f(r) == g(c)


def head16(i):
    return i >> 4


def in16(i):
    return i & 15


def lane_head(i):
    return i & 7


def lane_slice(i):
    return i >> 3


def same(i):
    return i


def block_slices(a16x32):
    rows = dot(match((WIDTH, D), in16, same).astype(BF16), a16x32).astype(BF16)
    wide = dot(rows, match((SLICES, LANES), same, lane_slice).astype(BF16))
    return jnp.where(match((WIDTH, LANES), head16, lane_head), wide, 0.0)


def block_square(a16x16):
    rows = dot(match((WIDTH, D), in16, same).astype(BF16), a16x16).astype(BF16)
    wide = dot(rows, match((D, WIDTH), same, in16).astype(BF16))
    return jnp.where(match((WIDTH, WIDTH), head16, head16), wide, 0.0)


def sharpness_row(sharp):
    col = lax.broadcasted_iota(jnp.int32, (1, LANES), 1) & 7
    row = jnp.zeros((1, LANES), F32)
    for h in range(HEADS):
        row = jnp.where(col == h, sharp[:, h : h + 1], row)
    return 1.0 / row


def parts(a):
    high = a.astype(BF16)
    return high, (a - high.astype(F32)).astype(BF16)


def head_sums():
    row, col = grid_of((2 * WIDTH, WIDTH))
    return ((row & 7) == (col & 7)).astype(BF16)


def group_sum(a, ones):
    high, low = parts(a[:, :WIDTH] + a[:, WIDTH:])
    return dot(jnp.concatenate([high, low], 1), ones)


def both_halves(a):
    return jnp.concatenate([a, a], 1)


def dot_left(a, b, cb=0):
    high, low = parts(a)
    return dot(jnp.concatenate([high, low], 1), jnp.concatenate([b, b], cb), 1, cb)


def dot_both(a, b, ca=1, cb=0):
    a_high, a_low = parts(a)
    b_high, b_low = parts(b)
    left = jnp.concatenate([a_high, a_high, a_low], ca)
    right = jnp.concatenate([b_high, b_low, b_high], cb)
    return dot(left, right, ca, cb)


def fold_lanes(a):
    for width in (64, 32, 16):
        a = a + pltpu.roll(a, width, 1)
    return a


def fold_rows(a, rows):
    return jnp.sum(a.reshape(a.shape[0] // rows, rows, a.shape[1]), 0)


def stack_heads(a):
    tall = jnp.broadcast_to(a[:, None, :], (SLICES, HEADS, WIDTH)).reshape(LANES, WIDTH)
    return jnp.where(match((LANES, WIDTH), lane_head, head16), tall, 0.0)


def unstack_heads(a):
    return jnp.sum(a.reshape(SLICES, HEADS, a.shape[1]), 1)


def pool_kernel(
    sharp, x, g, hidden, aggregate, offset, assign, result, rows_out, pool_out,
    weights, assign_wide, scale, ones, pooled, mass,
):
    step = pl.program_id(0)

    @pl.when(step == 0)
    def _():
        weights[:, :WIDTH] = hidden[...]
        weights[:, WIDTH:] = aggregate[...]
        assign_wide[...] = block_slices(assign[...]).astype(BF16)
        scale[...] = sharpness_row(sharp[...])
        ones[...] = head_sums()
        pooled[...] = jnp.zeros_like(pooled)
        mass[...] = jnp.zeros_like(mass)

    both = dot(x[...], weights[...])
    mid = both[:, :WIDTH].astype(BF16)
    feat = (both[:, WIDTH:] + offset[...]).astype(BF16)
    back = dot(g[...], result[...], 1, 1).astype(BF16)
    rows_out[:, :WIDTH] = mid
    rows_out[:, WIDTH : 2 * WIDTH] = back
    rows_out[:, 2 * WIDTH :] = feat
    expon = jnp.exp(dot(mid, assign_wide[...]) * scale[...])
    probs = expon * both_halves(1.0 / group_sum(expon, ones[...]))
    mass[...] += fold_rows(probs, 8)
    pooled[...] += dot(probs.astype(BF16), jnp.concatenate([back, feat], 1), 0, 0)

    @pl.when(step == pl.num_programs(0) - 1)
    def _():
        row, col = grid_of((LANES, LANES))
        small = unstack_heads(jnp.where((row & 7) == ((col & 127) >> 4), pooled[...], 0.0))
        total = jnp.sum(mass[...], 0, keepdims=True)
        for z in range(2):
            pool_out[2 * z, :SLICES] = small[:, WIDTH:]
            pool_out[2 * z, SLICES:] = total[:, :WIDTH]
            pool_out[2 * z + 1, :SLICES] = small[:, :WIDTH]
            pool_out[2 * z + 1, SLICES:] = total[:, WIDTH:]


def attend_terms(pool, ask, look, content, ones):
    numer = pool[0, :SLICES]
    token_grad = pool[1, :SLICES]
    mass = jnp.concatenate([pool[0, SLICES:], pool[1, SLICES:]], 1)
    spread = jnp.where(match((SLICES, LANES), same, lane_slice), mass, 0.0)
    heads = match((LANES, WIDTH), lane_head, head16)
    heads_half = heads.astype(BF16)
    high, low = parts(spread)
    rest = (spread - high.astype(F32) - low.astype(F32)).astype(BF16)
    denom = dot(jnp.concatenate([high, low, rest], 1), jnp.concatenate([heads_half] * 3, 0)) + EPS
    inverse = 1.0 / denom
    tokens = numer * inverse
    maps = jnp.concatenate([block_square(m[...]) for m in (ask, look, content)], 1).astype(BF16)
    q_k_v = dot_left(tokens, maps)
    q = q_k_v[:, :WIDTH]
    keys = stack_heads(q_k_v[:, WIDTH : 2 * WIDTH])
    values = stack_heads(q_k_v[:, 2 * WIDTH :])
    expon = jnp.exp(dot_both(q, keys, 1, 1) * 0.25)
    rows_back = dot_both(token_grad, values, 1, 1)
    rows = expon * both_halves(1.0 / group_sum(expon, ones))
    token_out = dot_both(rows, values)
    centre = both_halves(group_sum(rows_back * rows, ones))
    scores_back = rows * (rows_back - centre) * 0.25
    q_back = dot_both(scores_back, keys)
    k_back = unstack_heads(jnp.where(heads, dot_both(scores_back, q, 0, 0), 0.0))
    v_back = unstack_heads(jnp.where(heads, dot_both(rows, token_grad, 0, 0), 0.0))
    three = jnp.concatenate([q_back, k_back, v_back], 1)
    tok_back = dot_left(three, maps, 1)
    numer_back = tok_back * inverse
    folded = dot_left(numer_back * tokens, heads_half, 1)
    folded = jnp.where(match((SLICES, LANES), same, lane_slice), folded, 0.0)
    denom_back = -jnp.sum(folded, 0, keepdims=True)
    row, col = grid_of((WIDTH, 3 * WIDTH))
    wide = jnp.where((row >> 4) == ((col & 127) >> 4), dot_both(tokens, three, 0, 0), 0.0)
    wide = fold_rows(wide, D)
    grads = [fold_lanes(wide[:, i * WIDTH : (i + 1) * WIDTH]) for i in range(3)]
    return token_out, numer_back, denom_back, grads


def back_kernel(
    sharp, pool, hidden, aggregate, assign, ask, look, content, x, g, rows_in,
    sense_out, grads_out,
    weights, assign_wide, scale, ones, token_wide, denom_back, small,
    sum_pair, sum_slice, sum_bias, sum_heat,
):
    step = pl.program_id(0)

    @pl.when(step == 0)
    def _():
        weights[:, :WIDTH] = hidden[...]
        weights[:, WIDTH:] = aggregate[...]
        assign_wide[...] = block_slices(assign[...]).astype(BF16)
        scale[...] = sharpness_row(sharp[...])
        ones[...] = head_sums()
        token_out, numer_back, shift, grads = attend_terms(pool, ask, look, content, ones[...])
        token_wide[:, :WIDTH] = stack_heads(token_out).astype(BF16)
        token_wide[:, WIDTH:] = stack_heads(numer_back).astype(BF16)
        denom_back[...] = shift
        small[...] = jnp.zeros_like(small)
        lane = lax.broadcasted_iota(jnp.int32, (D, WIDTH), 1)
        for i, term in enumerate(grads):
            small[:D, :] += jnp.where((lane >> 4) == i, term, 0.0) * (1.0 / 64.0)
        for ref in (sum_pair, sum_slice, sum_bias, sum_heat):
            ref[...] = jnp.zeros_like(ref)

    mid = rows_in[:, :WIDTH]
    logits = dot(mid, assign_wide[...]) * scale[...]
    expon = jnp.exp(logits)
    probs = expon * both_halves(1.0 / group_sum(expon, ones[...]))
    prob_back = dot(rows_in[:, WIDTH:], token_wide[...], 1, 1) + denom_back[...]
    inner = both_halves(group_sum(probs * prob_back, ones[...]))
    logit_back = probs * (prob_back - inner)
    sum_heat[...] += fold_rows(logit_back * logits, 8)
    score_back = (logit_back * scale[...]).astype(BF16)
    mid_back = dot(score_back, assign_wide[...], 1, 1).astype(BF16)
    spread = dot(probs.astype(BF16), token_wide[...])
    mixed = spread[:, :WIDTH].astype(BF16)
    feat_wide = spread[:, WIDTH:]
    feat_back = feat_wide.astype(BF16)
    sum_bias[...] += fold_rows(feat_wide, 8)
    sense_out[...] = dot(jnp.concatenate([mid_back, feat_back], 1), weights[...], 1, 1)
    sum_slice[...] += dot(jnp.concatenate([x[...], mid], 1), score_back, 0, 0)
    sum_pair[...] += dot(
        jnp.concatenate([x[...], mixed], 1), jnp.concatenate([feat_back, g[...]], 1), 0, 0
    )

    @pl.when(step == pl.num_programs(0) - 1)
    def _():
        mid_grad = dot_left(sum_slice[:WIDTH], assign_wide[...], 1)
        kept = jnp.where(match((WIDTH, LANES), head16, lane_head), sum_slice[WIDTH:], 0.0)
        row, col = grid_of((LANES, WIDTH))
        kept = dot_left(fold_rows(kept, D), ((row >> 3) + 64 == col).astype(BF16))
        small[:D, :] += kept
        small[D : D + 1, :] = jnp.sum(sum_bias[...], 0, keepdims=True)
        heat = jnp.sum(sum_heat[...], 0, keepdims=True) * scale[...]
        heat = jnp.broadcast_to(heat[:, :WIDTH] + heat[:, WIDTH:], (8, WIDTH))
        for width in (64, 32, 16, 8):
            heat = heat + pltpu.roll(heat, width, 1)
        small[D + 1 : D + 2, :] = -heat[:1]
        sum_slice[:WIDTH, :WIDTH] = mid_grad
        for k in range(64):
            two = slice(2 * k, 2 * k + 2)
            low = slice(WIDTH + 2 * k, WIDTH + 2 * k + 2)
            grads_out[k, 0:2, :] = sum_slice[two, :WIDTH]
            grads_out[k, 2:4, :] = sum_pair[two, :WIDTH]
            grads_out[k, 4:6, :] = sum_pair[low, WIDTH:]
            grads_out[k, 6:8, :] = small[two, :]


def split_kernel(
    grads, mid_out, feat_out, bias_out, slice_out, heat_out, ask_out, look_out, content_out,
    result_out, small,
):
    for k in range(64):
        two = slice(2 * k, 2 * k + 2)
        mid_out[two, :] = grads[k, 0:2, :]
        feat_out[two, :] = grads[k, 2:4, :]
        result_out[two, :] = grads[k, 4:6, :]
        if k < 9:
            small[two, :] = grads[k, 6:8, :]
    ask_out[...] = small[:D, 0:D]
    look_out[...] = small[:D, D : 2 * D]
    content_out[...] = small[:D, 2 * D : 3 * D]
    slice_out[...] = small[:D, 64 : 64 + SLICES]
    bias_out[...] = small[D : D + 1, :]
    heat_out[...] = small[D + 1 : D + 2, :HEADS]


def exchange(block, axes, copies):
    sent = jnp.broadcast_to(block[None], (copies,) + block.shape)
    return lax.all_to_all(sent, axes, 0, 0, tiled=True)


def sum_over_nodes(sent):
    part = jnp.sum(lax.all_to_all(sent, ("zh", "core"), 0, 0, tiled=True), 0)
    part = jnp.sum(exchange(part, ("y", "x"), 16), 0)
    return lax.all_gather(part, "core", axis=0, tiled=False)


def sum_over_all(sent):
    part = jnp.sum(lax.all_to_all(sent, BLOCK, 0, 0, tiled=True), 0)
    part = jnp.sum(exchange(part, COLUMN, 8), 0)
    return exchange(part, BLOCK, 64)


def whole(shape):
    return pl.BlockSpec(shape, lambda i: (0,) * len(shape))


def tiled(width):
    return pl.BlockSpec((TILE, width), lambda i: (i, 0))


def hbm(a):
    return pltpu.with_memory_space_constraint(a, pltpu.HBM)


def shape(dims, dtype=F32):
    return jax.ShapeDtypeStruct(dims, dtype)


def pool(x, g, hidden, aggregate, offset, assign, sharp, result):
    nodes = x.shape[0]
    return pl.pallas_call(
        pool_kernel,
        grid=(nodes // TILE,),
        in_specs=[
            whole((1, HEADS)),
            tiled(WIDTH), tiled(WIDTH), whole((WIDTH, WIDTH)), whole((WIDTH, WIDTH)),
            whole((1, WIDTH)), whole((D, SLICES)), whole((WIDTH, WIDTH)),
        ],
        out_specs=[tiled(3 * WIDTH), whole((4, SLICES + 1, 128))],
        out_shape=[
            shape((nodes, 3 * WIDTH), BF16), shape((4, SLICES + 1, 128)),
        ],
        scratch_shapes=[
            pltpu.VMEM((WIDTH, LANES), BF16), pltpu.VMEM((WIDTH, LANES), BF16),
            pltpu.VMEM((1, LANES), F32), pltpu.VMEM((LANES, WIDTH), BF16),
            pltpu.VMEM((LANES, LANES), F32), pltpu.VMEM((8, LANES), F32),
        ],
        compiler_params=pltpu.CompilerParams(vmem_limit_bytes=40 << 20),
        name="pool",
    )(*[hbm(a) for a in (sharp, x, g, hidden, aggregate, offset, assign, result)])


def back(pool_sum, x, g, hidden, aggregate, assign, sharp, ask, look, content, rows):
    nodes = x.shape[0]
    return pl.pallas_call(
        back_kernel,
        grid=(nodes // TILE,),
        in_specs=[
            whole((1, HEADS)), whole((2, SLICES + 1, 128)),
            whole((WIDTH, WIDTH)), whole((WIDTH, WIDTH)), whole((D, SLICES)),
            whole((D, D)), whole((D, D)), whole((D, D)),
            tiled(WIDTH), tiled(WIDTH), tiled(3 * WIDTH),
        ],
        out_specs=[tiled(WIDTH), whole((64, 8, 128))],
        out_shape=[shape((nodes, WIDTH)), shape((64, 8, 128))],
        scratch_shapes=[
            pltpu.VMEM((WIDTH, LANES), BF16), pltpu.VMEM((WIDTH, LANES), BF16),
            pltpu.VMEM((1, LANES), F32), pltpu.VMEM((LANES, WIDTH), BF16),
            pltpu.VMEM((LANES, LANES), BF16), pltpu.VMEM((1, LANES), F32),
            pltpu.VMEM((WIDTH, WIDTH), F32), pltpu.VMEM((LANES, LANES), F32),
            pltpu.VMEM((LANES, LANES), F32),
            pltpu.VMEM((8, WIDTH), F32), pltpu.VMEM((8, LANES), F32),
        ],
        compiler_params=pltpu.CompilerParams(vmem_limit_bytes=40 << 20),
        name="back",
    )(hbm(sharp), pool_sum, *[hbm(a) for a in (hidden, aggregate, assign, ask, look, content, x, g)], rows)


def split(grads):
    square = (WIDTH, WIDTH)
    outs = [
        square, square, (1, WIDTH), (D, SLICES), (1, HEADS), (D, D), (D, D), (D, D), square,
    ]
    return pl.pallas_call(
        split_kernel,
        out_shape=[shape(s) for s in outs],
        scratch_shapes=[pltpu.VMEM((32, 128), F32)],
        name="split",
    )(grads)


def shards(
    vertex_embedding_array,
    result_sensitivity,
    hidden_projection,
    aggregate_projection,
    aggregate_offset,
    assignment_projection,
    softmax_sharpness,
    state_asking_map,
    state_lookup_map,
    state_content_map,
    result_projection,
):
    x = vertex_embedding_array[0]
    g = result_sensitivity[0]
    rows, pooled = pool(
        x, g, hidden_projection, aggregate_projection, aggregate_offset[None],
        assignment_projection, softmax_sharpness[None], result_projection,
    )
    pool_sum = sum_over_nodes(pooled)
    sense, grads = back(
        pool_sum, x, g, hidden_projection, aggregate_projection, assignment_projection,
        softmax_sharpness[None], state_asking_map, state_lookup_map, state_content_map, rows,
    )
    mid, feat, bias, slices, heat, ask, look, content, result = split(sum_over_all(grads))
    return sense[None], mid, feat, bias[0], slices, heat[0], ask, look, content, result


def solution(mesh):
    fine = Mesh(mesh.devices.reshape(2, 2, 2, 4, 2, 4, 2), MEMBER + NODE)
    nodes = P(MEMBER, NODE, None)
    return jax.shard_map(
        shards,
        mesh=fine,
        in_specs=(nodes, nodes) + (P(),) * 9,
        out_specs=(nodes,) + (P(),) * 9,
        check_vma=False,
    )
```

time: 127 us -> 110 us (0.87)
  local copies, waits for them, and re-layouts: 10.4 us -> 0.05 us
  Pallas kernels: 22.7 us -> 16.9 us
    unnamed x38 -> x0, local copies, waits for them, and re-layouts: 10.3 us -> none
    pallas_call x2, Pallas kernels: 21 us -> 15.3 us  [the longest x1 10.3 us: back(): pl.pallas_call(back_kernel, grid=(nodes // TILE,), in_specs=[whole((1, HE...]
    all_to_all x3, blocking collectives: 47.9 us -> 45.9 us  [exchange(): return lax.all_to_all(sent, axes, 0, 0, tiled=True)]
    all_to_all x1, blocking collectives: 12.1 us -> 13.8 us  [sum_over_all(): part = jnp.sum(lax.all_to_all(sent, BLOCK, 0, 0, tiled=True), 0)]
where the time goes in v3:
time: 110 us
  blocking collectives  91.8 us (83%)
  Pallas kernels  16.9 us (15%)
    all_to_all x3, blocking collectives, exchange(): return lax.all_to_all(sent, axes, 0, 0, tiled=True)  45.9 us
    all_to_all x1, blocking collectives, sum_over_nodes(): part = jnp.sum(lax.all_to_all(sent, ('zh', 'core'), 0, 0, tiled=True), 0)  28.4 us
    all_to_all x1, blocking collectives, sum_over_all(): part = jnp.sum(lax.all_to_all(sent, BLOCK, 0, 0, tiled=True), 0)  13.8 us
    pallas_call x1, Pallas kernels, back(): pl.pallas_call(back_kernel, grid=(nodes // TILE,), in_specs=[whole((1, HE...  10.3 us
    pallas_call x1, Pallas kernels, pool(): pl.pallas_call(pool_kernel, grid=(nodes // TILE,), in_specs=[whole((1, HE...  4.92 us
    all_gather x1, blocking collectives, sum_over_nodes(): return lax.all_gather(part, 'core', axis=0, tiled=False)  3.72 us

profile of v3, /device:TPU:1, one launch (start us, length us, event | category | flops | bytes accessed | tf_op | source)
XLA Modules:
  0.0 109.6 jit_solution(17425031428379272801)
XLA Ops:
  0.6 4.9 %pool.1 = (bf16[4096,384]{1,0:T(8,128)(2,1)S(1)}, f32[4,33,128]{2,1,0:T(8,128)S(1)}) custom-call(f32[1,8]{1,0:T(1,128)} %bitcast.13, bf16[4096,128]{1,0:T(8,128)(2,1)} %bitcast.8, bf16[4096,128]{1,0:T(8,128)(2,1)} %bitcast.10, bf16[128,128]{1,0:T(8,128)(2,1)} %hidden.3, bf16[128,128]{1,0:T(8,128)(2,1)} %aggregate.3, f32[1,128]{1,0:T(1,128)} %bitcast.15, ...), custom_call_target="tpu_custom_call" | custom-call | tf_op jit(solution)/shard_map/pool/pallas_call | solution.py:332
  5.6 28.4 %all_to_all.25 = f32[4,33,128]{2,1,0:T(8,128)S(1)} all-to-all(f32[4,33,128]{2,1,0:T(8,128)S(1)} %get-tuple-element.23), channel_id=1, replica_groups=mesh['z4'=2,'z2'=2,'z1'=2,'y'=4,'zh'=2,'x'=4,'core'=2] {'zh','core'}, dimensions={0} | all-to-all | bytes 135168 | tf_op jit(solution)/shard_map/all_to_all | solution.py:303
  34.0 14.7 %all_to_all.26 = f32[16,33,128]{2,1,0:T(8,128)S(1)} all-to-all(f32[16,33,128]{2,1,0:T(8,128)S(1)} %broadcast_in_dim.14), channel_id=1, replica_groups=mesh['z4'=2,'z2'=2,'z1'=2,'y'=4,'zh'=2,'x'=4,'core'=2] {'y','x'}, dimensions={0} | all-to-all | bytes 540672 | tf_op jit(solution)/shard_map/all_to_all | solution.py:299
  48.7 3.7 %all-gather.1.pool = f32[2,33,128]{2,1,0:T(8,128)S(1)} all-gather(f32[1,33,128]{2,1,0:T(8,128)S(1)} %bitcast.12), channel_id=2, replica_groups=mesh['z4'=2,'z2'=2,'z1'=2,'y'=4,'zh'=2,'x'=4,'core'=2] {'core'}, dimensions={0}, use_global_device_ids=true | all-gather | bytes 50688 | tf_op jit(solution)/shard_map/all_gather | solution.py:305
  52.4 10.3 %back.1 = (f32[4096,128]{1,0:T(8,128)}, f32[64,8,128]{2,1,0:T(8,128)S(1)}) custom-call(f32[1,8]{1,0:T(1,128)} %bitcast.14, f32[2,33,128]{2,1,0:T(8,128)S(1)} %all-gather.1.pool, bf16[128,128]{1,0:T(8,128)(2,1)} %hidden.3, bf16[128,128]{1,0:T(8,128)(2,1)} %aggregate.3, bf16[16,32]{1,0:T(8,128)(2,1)} %assign.3, bf16[16,16]{1,0:T(8,128)(2,1)} %ask.1, ...), custom_call_target="tpu_custom_call" | custom-call | tf_op jit(solution)/shard_map/back/pallas_call | solution.py:356
  62.8 13.8 %all_to_all.27 = f32[64,8,128]{2,1,0:T(8,128)S(1)} all-to-all(f32[64,8,128]{2,1,0:T(8,128)S(1)} %get-tuple-element.26), channel_id=1, replica_groups=mesh['z4'=2,'z2'=2,'z1'=2,'y'=4,'zh'=2,'x'=4,'core'=2] {'z1','y','x','co..., dimensions={0} | all-to-all | bytes 524288 | tf_op jit(solution)/shard_map/all_to_all | solution.py:309
  76.6 0.1 reduce_sum.38
  76.7 15.5 %all_to_all.28 = f32[8,8,128]{2,1,0:T(8,128)S(1)} all-to-all(f32[8,8,128]{2,1,0:T(8,128)S(1)} %broadcast_in_dim.32), channel_id=1, replica_groups=mesh['z4'=2,'z2'=2,'z1'=2,'y'=4,'zh'=2,'x'=4,'core'=2] {'z4','z2','zh'}, dimensions={0} | all-to-all | bytes 65536 | tf_op jit(solution)/shard_map/all_to_all | solution.py:299
  92.2 15.7 %all_to_all.29.grads = f32[64,8,128]{2,1,0:T(8,128)} all-to-all(f32[64,8,128]{2,1,0:T(8,128)S(1)} %broadcast_in_dim.33), channel_id=1, replica_groups=mesh['z4'=2,'z2'=2,'z1'=2,'y'=4,'zh'=2,'x'=4,'core'=2] {'z1','y','x','co..., dimensions={0} | all-to-all | bytes 524288 | tf_op jit(solution)/shard_map/all_to_all | solution.py:299
  107.9 1.7 %split.1 = (f32[128,128]{1,0:T(8,128)}, f32[128,128]{1,0:T(8,128)}, f32[1,128]{1,0:T(1,128)}, f32[16,32]{1,0:T(8,128)}, f32[1,8]{1,0:T(1,128)}, /*index=5*/f32[1...) custom-call(f32[64,8,128]{2,1,0:T(8,128)} %all_to_all.29.grads), custom_call_target="tpu_custom_call" | custom-call | tf_op jit(solution)/shard_map/split/pallas_call | solution.py:385
  (6 shorter events, 0.1 us)

commit v4 on v3

--- a/solution.py
+++ b/solution.py
@@ -12,6 +12,7 @@
 LANES = HEADS * SLICES
 EPS = 1e-05
 TILE = 2048
+GRAD_ROWS = 512
 MEMBER = ("z4", "z2", "z1")
 NODE = ("y", "zh", "x", "core")
 BLOCK = ("z1", "y", "x", "core")
@@ -164,6 +165,32 @@
             pool_out[2 * z, SLICES:] = total[:, :WIDTH]
             pool_out[2 * z + 1, :SLICES] = small[:, :WIDTH]
             pool_out[2 * z + 1, SLICES:] = total[:, WIDTH:]
+
+
+def cross_kernel(
+    sharp, assign, x, g, rows_in, probs_out, cross_out, assign_wide, scale, ones, mass,
+):
+    step = pl.program_id(0)
+
+    @pl.when(step == 0)
+    def _():
+        assign_wide[...] = block_slices(assign[...]).astype(BF16)
+        scale[...] = sharpness_row(sharp[...])
+        ones[...] = head_sums()
+        cross_out[...] = jnp.zeros_like(cross_out)
+        mass[...] = jnp.zeros_like(mass)
+
+    expon = jnp.exp(dot(rows_in[:, :WIDTH], assign_wide[...]) * scale[...])
+    probs = expon * both_halves(1.0 / group_sum(expon, ones[...]))
+    probs_out[...] = probs
+    half = probs.astype(BF16)
+    mass[...] += fold_rows(half.astype(F32), 8)
+    cross_out[:LANES] += dot(half, jnp.concatenate([x[...], g[...]], 1), 0, 0)
+
+    @pl.when(step == pl.num_programs(0) - 1)
+    def _():
+        total = jnp.sum(mass[...], 0, keepdims=True)
+        cross_out[LANES:] = jnp.broadcast_to(total, (8, LANES))
 
 
 def attend_terms(pool, ask, look, content, ones):
@@ -206,17 +233,27 @@
 
 
 def back_kernel(
-    sharp, pool, hidden, aggregate, assign, ask, look, content, x, g, rows_in,
-    sense_out, grads_out,
-    weights, assign_wide, scale, ones, token_wide, denom_back, small,
-    sum_pair, sum_slice, sum_bias, sum_heat,
+    sharp, assign, ask, look, content, pool, cross, rows_in, x_hbm, probs_hbm,
+    score_hbm, numer_out, grads_out,
+    x, probs_all, score_all, assign_wide, scale, ones, token_wide, denom_back, small, sum_slice, sum_heat,
+    sems, out_sems,
 ):
     step = pl.program_id(0)
+    last = pl.num_programs(0) - 1
+    tiles = x.shape[0] // TILE
+
+    def fetches(i):
+        t = slice(i * TILE, (i + 1) * TILE)
+        return [
+            pltpu.make_async_copy(probs_hbm.at[t], probs_all.at[t], sems.at[2 * i]),
+            pltpu.make_async_copy(x_hbm.at[t], x.at[t], sems.at[2 * i + 1]),
+        ]
 
     @pl.when(step == 0)
     def _():
-        weights[:, :WIDTH] = hidden[...]
-        weights[:, WIDTH:] = aggregate[...]
+        for i in range(tiles):
+            for copy in fetches(i):
+                copy.start()
         assign_wide[...] = block_slices(assign[...]).astype(BF16)
         scale[...] = sharpness_row(sharp[...])
         ones[...] = head_sums()
@@ -228,64 +265,90 @@
         lane = lax.broadcasted_iota(jnp.int32, (D, WIDTH), 1)
         for i, term in enumerate(grads):
             small[:D, :] += jnp.where((lane >> 4) == i, term, 0.0) * (1.0 / 64.0)
-        for ref in (sum_pair, sum_slice, sum_bias, sum_heat):
-            ref[...] = jnp.zeros_like(ref)
-
+        sum_slice[...] = jnp.zeros_like(sum_slice)
+        sum_heat[...] = jnp.zeros_like(sum_heat)
+
+    def sends(i):
+        t = slice(i * TILE, (i + 1) * TILE)
+        return pltpu.make_async_copy(score_all.at[t], score_hbm.at[t], out_sems.at[i])
+
+    for i in range(tiles):
+
+        @pl.when(step == i)
+        def _(i=i):
+            for copy in fetches(i):
+                copy.wait()
+
+    here = pl.ds(pl.multiple_of(step * TILE, TILE), TILE)
     mid = rows_in[:, :WIDTH]
+    probs = probs_all[here]
     logits = dot(mid, assign_wide[...]) * scale[...]
-    expon = jnp.exp(logits)
-    probs = expon * both_halves(1.0 / group_sum(expon, ones[...]))
     prob_back = dot(rows_in[:, WIDTH:], token_wide[...], 1, 1) + denom_back[...]
     inner = both_halves(group_sum(probs * prob_back, ones[...]))
     logit_back = probs * (prob_back - inner)
     sum_heat[...] += fold_rows(logit_back * logits, 8)
     score_back = (logit_back * scale[...]).astype(BF16)
-    mid_back = dot(score_back, assign_wide[...], 1, 1).astype(BF16)
-    spread = dot(probs.astype(BF16), token_wide[...])
-    mixed = spread[:, :WIDTH].astype(BF16)
-    feat_wide = spread[:, WIDTH:]
-    feat_back = feat_wide.astype(BF16)
-    sum_bias[...] += fold_rows(feat_wide, 8)
-    sense_out[...] = dot(jnp.concatenate([mid_back, feat_back], 1), weights[...], 1, 1)
-    sum_slice[...] += dot(jnp.concatenate([x[...], mid], 1), score_back, 0, 0)
-    sum_pair[...] += dot(
-        jnp.concatenate([x[...], mixed], 1), jnp.concatenate([feat_back, g[...]], 1), 0, 0
-    )
-
-    @pl.when(step == pl.num_programs(0) - 1)
+    score_all[here] = score_back
+    for i in range(tiles):
+
+        @pl.when(step == i)
+        def _(i=i):
+            sends(i).start()
+
+    sum_slice[...] += dot(jnp.concatenate([x[here], mid], 1), score_back, 0, 0)
+
+    @pl.when(step == last)
     def _():
         mid_grad = dot_left(sum_slice[:WIDTH], assign_wide[...], 1)
+        tokens = token_wide[:, :WIDTH]
+        numers = token_wide[:, WIDTH:]
+        cross_high, cross_low = parts(cross[:LANES])
+        feat_grad = dot(cross_high[:, :WIDTH], numers, 0, 0) + dot(
+            cross_low[:, :WIDTH], numers, 0, 0
+        )
+        result_grad = dot(tokens, cross_high[:, WIDTH:], 0, 0) + dot(
+            tokens, cross_low[:, WIDTH:], 0, 0
+        )
+        mass_high, mass_low = parts(cross[LANES:])
+        mass_rest = (
+            cross[LANES:] - mass_high.astype(F32) - mass_low.astype(F32)
+        ).astype(BF16)
+        bias_grad = dot(mass_high, numers) + dot(mass_low, numers) + dot(mass_rest, numers)
         kept = jnp.where(match((WIDTH, LANES), head16, lane_head), sum_slice[WIDTH:], 0.0)
         row, col = grid_of((LANES, WIDTH))
         kept = dot_left(fold_rows(kept, D), ((row >> 3) + 64 == col).astype(BF16))
         small[:D, :] += kept
-        small[D : D + 1, :] = jnp.sum(sum_bias[...], 0, keepdims=True)
+        small[D : D + 1, :] = bias_grad[:1]
         heat = jnp.sum(sum_heat[...], 0, keepdims=True) * scale[...]
         heat = jnp.broadcast_to(heat[:, :WIDTH] + heat[:, WIDTH:], (8, WIDTH))
         for width in (64, 32, 16, 8):
             heat = heat + pltpu.roll(heat, width, 1)
         small[D + 1 : D + 2, :] = -heat[:1]
-        sum_slice[:WIDTH, :WIDTH] = mid_grad
-        for k in range(64):
-            two = slice(2 * k, 2 * k + 2)
-            low = slice(WIDTH + 2 * k, WIDTH + 2 * k + 2)
-            grads_out[k, 0:2, :] = sum_slice[two, :WIDTH]
-            grads_out[k, 2:4, :] = sum_pair[two, :WIDTH]
-            grads_out[k, 4:6, :] = sum_pair[low, WIDTH:]
-            grads_out[k, 6:8, :] = small[two, :]
+        numer_out[...] = numers
+        grads_out[:WIDTH] = mid_grad
+        grads_out[WIDTH : 2 * WIDTH] = feat_grad
+        grads_out[2 * WIDTH : 3 * WIDTH] = result_grad
+        grads_out[3 * WIDTH :] = small[...]
+        for i in range(tiles):
+            sends(i).wait()
+
+
+def sense_kernel(hidden, aggregate, assign, numers, score, probs, sense_out):
+    weights = jnp.concatenate([hidden[...], aggregate[...]], 1)
+    assign_wide = block_slices(assign[...]).astype(BF16)
+    mid_back = dot(score[...], assign_wide, 1, 1).astype(BF16)
+    feat_back = dot(probs[...].astype(BF16), numers[...]).astype(BF16)
+    sense_out[...] = dot(jnp.concatenate([mid_back, feat_back], 1), weights, 1, 1)
 
 
 def split_kernel(
     grads, mid_out, feat_out, bias_out, slice_out, heat_out, ask_out, look_out, content_out,
-    result_out, small,
+    result_out,
 ):
-    for k in range(64):
-        two = slice(2 * k, 2 * k + 2)
-        mid_out[two, :] = grads[k, 0:2, :]
-        feat_out[two, :] = grads[k, 2:4, :]
-        result_out[two, :] = grads[k, 4:6, :]
-        if k < 9:
-            small[two, :] = grads[k, 6:8, :]
+    mid_out[...] = grads[:WIDTH]
+    feat_out[...] = grads[WIDTH : 2 * WIDTH]
+    result_out[...] = grads[2 * WIDTH : 3 * WIDTH]
+    small = grads[3 * WIDTH : 3 * WIDTH + 24]
     ask_out[...] = small[:D, 0:D]
     look_out[...] = small[:D, D : 2 * D]
     content_out[...] = small[:D, 2 * D : 3 * D]
@@ -306,9 +369,10 @@
 
 
 def sum_over_all(sent):
+    sent = sent.reshape(64, GRAD_ROWS // 64, 128)
     part = jnp.sum(lax.all_to_all(sent, BLOCK, 0, 0, tiled=True), 0)
     part = jnp.sum(exchange(part, COLUMN, 8), 0)
-    return exchange(part, BLOCK, 64)
+    return exchange(part, BLOCK, 64).reshape(GRAD_ROWS, 128)
 
 
 def whole(shape):
@@ -351,30 +415,70 @@
     )(*[hbm(a) for a in (sharp, x, g, hidden, aggregate, offset, assign, result)])
 
 
-def back(pool_sum, x, g, hidden, aggregate, assign, sharp, ask, look, content, rows):
+def cross(x, g, assign, sharp, rows):
+    nodes = x.shape[0]
+    return pl.pallas_call(
+        cross_kernel,
+        grid=(nodes // TILE,),
+        in_specs=[
+            whole((1, HEADS)), whole((D, SLICES)), tiled(WIDTH), tiled(WIDTH), tiled(3 * WIDTH),
+        ],
+        out_specs=[tiled(LANES), whole((LANES + 8, LANES))],
+        out_shape=[pltpu.HBM((nodes, LANES), F32), shape((LANES + 8, LANES))],
+        scratch_shapes=[
+            pltpu.VMEM((WIDTH, LANES), BF16), pltpu.VMEM((1, LANES), F32),
+            pltpu.VMEM((LANES, WIDTH), BF16), pltpu.VMEM((8, LANES), F32),
+        ],
+        compiler_params=pltpu.CompilerParams(vmem_limit_bytes=40 << 20),
+        name="cross",
+    )(hbm(sharp), hbm(assign), hbm(x), hbm(g), rows)
+
+
+def back(pool_sum, crossed, x, assign, sharp, ask, look, content, probs, rows):
     nodes = x.shape[0]
     return pl.pallas_call(
         back_kernel,
         grid=(nodes // TILE,),
         in_specs=[
-            whole((1, HEADS)), whole((2, SLICES + 1, 128)),
-            whole((WIDTH, WIDTH)), whole((WIDTH, WIDTH)), whole((D, SLICES)),
-            whole((D, D)), whole((D, D)), whole((D, D)),
-            tiled(WIDTH), tiled(WIDTH), tiled(3 * WIDTH),
-        ],
-        out_specs=[tiled(WIDTH), whole((64, 8, 128))],
-        out_shape=[shape((nodes, WIDTH)), shape((64, 8, 128))],
+            whole((1, HEADS)), whole((D, SLICES)), whole((D, D)), whole((D, D)), whole((D, D)),
+            whole((2, SLICES + 1, 128)), whole((LANES + 8, LANES)), tiled(3 * WIDTH),
+            pl.BlockSpec(memory_space=pltpu.HBM), pl.BlockSpec(memory_space=pltpu.HBM),
+        ],
+        out_specs=[
+            pl.BlockSpec(memory_space=pltpu.HBM), whole((LANES, WIDTH)), whole((GRAD_ROWS, 128)),
+        ],
+        out_shape=[
+            pltpu.HBM((nodes, LANES), BF16), shape((LANES, WIDTH), BF16), shape((GRAD_ROWS, 128)),
+        ],
         scratch_shapes=[
-            pltpu.VMEM((WIDTH, LANES), BF16), pltpu.VMEM((WIDTH, LANES), BF16),
-            pltpu.VMEM((1, LANES), F32), pltpu.VMEM((LANES, WIDTH), BF16),
-            pltpu.VMEM((LANES, LANES), BF16), pltpu.VMEM((1, LANES), F32),
-            pltpu.VMEM((WIDTH, WIDTH), F32), pltpu.VMEM((LANES, LANES), F32),
-            pltpu.VMEM((LANES, LANES), F32),
-            pltpu.VMEM((8, WIDTH), F32), pltpu.VMEM((8, LANES), F32),
+            pltpu.VMEM((nodes, WIDTH), BF16), pltpu.VMEM((nodes, LANES), F32),
+            pltpu.VMEM((nodes, LANES), BF16),
+            pltpu.VMEM((WIDTH, LANES), BF16), pltpu.VMEM((1, LANES), F32),
+            pltpu.VMEM((LANES, WIDTH), BF16), pltpu.VMEM((LANES, LANES), BF16),
+            pltpu.VMEM((1, LANES), F32), pltpu.VMEM((WIDTH, WIDTH), F32),
+            pltpu.VMEM((LANES, LANES), F32), pltpu.VMEM((8, LANES), F32),
+            pltpu.SemaphoreType.DMA((2 * (nodes // TILE),)),
+            pltpu.SemaphoreType.DMA((nodes // TILE,)),
         ],
         compiler_params=pltpu.CompilerParams(vmem_limit_bytes=40 << 20),
         name="back",
-    )(hbm(sharp), pool_sum, *[hbm(a) for a in (hidden, aggregate, assign, ask, look, content, x, g)], rows)
+    )(sharp, assign, ask, look, content, pool_sum, crossed, rows, hbm(x), hbm(probs))
+
+
+def sense(hidden, aggregate, assign, numers, score, probs):
+    nodes = score.shape[0]
+    square = whole((WIDTH, WIDTH))
+    return pl.pallas_call(
+        sense_kernel,
+        grid=(nodes // TILE,),
+        in_specs=[
+            square, square, whole((D, SLICES)), whole((LANES, WIDTH)), tiled(LANES), tiled(LANES),
+        ],
+        out_specs=tiled(WIDTH),
+        out_shape=pltpu.HBM((nodes, WIDTH), F32),
+        compiler_params=pltpu.CompilerParams(vmem_limit_bytes=40 << 20),
+        name="sense",
+    )(*[hbm(a) for a in (hidden, aggregate, assign)], numers, hbm(score), hbm(probs))
 
 
 def split(grads):
@@ -385,9 +489,8 @@
     return pl.pallas_call(
         split_kernel,
         out_shape=[shape(s) for s in outs],
-        scratch_shapes=[pltpu.VMEM((32, 128), F32)],
         name="split",
-    )(grads)
+    )(pltpu.with_memory_space_constraint(grads, pltpu.VMEM))
 
 
 def shards(
@@ -409,13 +512,18 @@
         x, g, hidden_projection, aggregate_projection, aggregate_offset[None],
         assignment_projection, softmax_sharpness[None], result_projection,
     )
+    sharp = softmax_sharpness[None]
     pool_sum = sum_over_nodes(pooled)
-    sense, grads = back(
-        pool_sum, x, g, hidden_projection, aggregate_projection, assignment_projection,
-        softmax_sharpness[None], state_asking_map, state_lookup_map, state_content_map, rows,
+    probs, crossed = cross(x, g, assignment_projection, sharp, rows)
+    score, numers, grads = back(
+        pool_sum, crossed, x, assignment_projection, sharp, state_asking_map, state_lookup_map,
+        state_content_map, probs, rows,
+    )
+    nodes_out = sense(
+        hidden_projection, aggregate_projection, assignment_projection, numers, score, probs
     )
     mid, feat, bias, slices, heat, ask, look, content, result = split(sum_over_all(grads))
-    return sense[None], mid, feat, bias[0], slices, heat[0], ask, look, content, result
+    return nodes_out[None], mid, feat, bias[0], slices, heat[0], ask, look, content, result
 
 
 def solution(mesh):

time: 110 us -> 108 us (0.982)
  blocking collectives: 91.8 us -> 61.6 us
  starting transfers between devices: 0 us -> 13 us
  waiting for transfers between devices: 0 us -> 7.03 us
  Pallas kernels: 16.9 us -> 22.6 us
  local copies, waits for them, and re-layouts: 0.05 us -> 1.51 us
    all_to_all x3 -> x1, blocking collectives: 45.9 us -> 15.4 us  [exchange(): return lax.all_to_all(sent, axes, 0, 0, tiled=True)]
    all_to_all x0 -> x2, starting transfers between devices: none -> 13 us  [exchange(): return lax.all_to_all(sent, axes, 0, 0, tiled=True)]
    pallas_call x1 -> x3, Pallas kernels: 1.67 us -> 11.6 us  [the longest x1 5.61 us: sense(): pl.pallas_call(sense_kernel, grid=(nodes // TILE,), in_specs=[square, squ...]
    all_to_all x0 -> x2, waiting for transfers between devices: none -> 7.03 us  [exchange(): return lax.all_to_all(sent, axes, 0, 0, tiled=True)]
    pallas_call x1, Pallas kernels: 10.3 us -> 6.04 us  [back(): pl.pallas_call(back_kernel, grid=(nodes // TILE,), in_specs=[whole((1, HE...]
    broadcast_in_dim x3, local copies, waits for them, and re-layouts: 0.05 us -> 1.49 us  [exchange(): sent = jnp.broadcast_to(block[None], (copies,) + block.shape)]
  transfers between devices with their start and end apart: 0 -> 2, of which waited for: 0 -> 2; matrix products, arithmetic and copies ran while one was open for 0% -> 0% of each run, Pallas kernels for 0% -> 10%
where the time goes in v4:
time: 108 us
  blocking collectives  61.6 us (57%)
  Pallas kernels  22.6 us (21%)
  starting transfers between devices  13 us (12%)
  waiting for transfers between devices  7.03 us (7%)
  local copies, waits for them, and re-layouts  1.51 us (1%)
  other arithmetic  1.09 us (1%)
    all_to_all x1, blocking collectives, sum_over_nodes(): part = jnp.sum(lax.all_to_all(sent, ('zh', 'core'), 0, 0, tiled=True), 0)  28.4 us
    all_to_all x1, blocking collectives, exchange(): return lax.all_to_all(sent, axes, 0, 0, tiled=True)  15.4 us
    all_to_all x1, blocking collectives, sum_over_all(): part = jnp.sum(lax.all_to_all(sent, BLOCK, 0, 0, tiled=True), 0)  14 us
    all_to_all x2, starting transfers between devices, exchange(): return lax.all_to_all(sent, axes, 0, 0, tiled=True)  13 us
    all_to_all x2, waiting for transfers between devices, exchange(): return lax.all_to_all(sent, axes, 0, 0, tiled=True)  7.03 us
    pallas_call x1, Pallas kernels, back(): pl.pallas_call(back_kernel, grid=(nodes // TILE,), in_specs=[whole((1, HE...  6.04 us
    pallas_call x1, Pallas kernels, sense(): pl.pallas_call(sense_kernel, grid=(nodes // TILE,), in_specs=[square, squ...  5.61 us
    pallas_call x1, Pallas kernels, cross(): pl.pallas_call(cross_kernel, grid=(nodes // TILE,), in_specs=[whole((1, H...  5.27 us
  transfers between devices with their start and end apart: 2, of which 2 were waited for; matrix products, arithmetic and copies ran while one was open for 0% of the time, Pallas kernels for 10%

profile of v4, /device:TPU:1, one launch (start us, length us, event | category | flops | bytes accessed | tf_op | source)
XLA Modules:
  0.0 107.5 jit_solution(6942803727435563531)
XLA Ops:
  0.6 4.9 %pool.1 = (bf16[4096,384]{1,0:T(8,128)(2,1)S(1)}, f32[4,33,128]{2,1,0:T(8,128)S(1)}) custom-call(f32[1,8]{1,0:T(1,128)} %bitcast.12, bf16[4096,128]{1,0:T(8,128)(2,1)} %bitcast.15, bf16[4096,128]{1,0:T(8,128)(2,1)} %bitcast.18, bf16[128,128]{1,0:T(8,128)(2,1)} %hidden.3, bf16[128,128]{1,0:T(8,128)(2,1)} %aggregate.3, f32[1,128]{1,0:T(1,128)} %bitcast.22, ...), custom_call_target="tpu_custom_call" | custom-call | tf_op jit(solution)/shard_map/pool/pallas_call | solution.py:396
  5.6 28.4 %all_to_all.25 = f32[4,33,128]{2,1,0:T(8,128)S(1)} all-to-all(f32[4,33,128]{2,1,0:T(8,128)S(1)} %get-tuple-element.26), channel_id=1, replica_groups=mesh['z4'=2,'z2'=2,'z1'=2,'y'=4,'zh'=2,'x'=4,'core'=2] {'zh','core'}, dimensions={0} | all-to-all | bytes 135168 | tf_op jit(solution)/shard_map/all_to_all | solution.py:366
  34.0 0.7 broadcast_in_dim.14
  34.7 0.0 copy-start
  34.7 0.0 copy-start.1
  34.7 0.0 copy-start.2
  34.7 0.0 copy-start.3
  34.7 0.0 copy-start.4
  34.8 6.9 %all-to-all-start.1 = ((f32[16,33,128]{2,1,0:T(8,128)}), f32[16,33,128]{2,1,0:T(8,128)}, u32[]{:S(2)}, u32[]{:S(2)}) async-start(f32[16,33,128]{2,1,0:T(8,128)} %broadcast_in_dim.14), calls=%async_computation.1 | async-start | bytes 655360 | tf_op jit(solution)/shard_map/all_to_all | solution.py:362
  41.7 5.3 %cross.1 = (f32[4096,256]{1,0:T(8,128)}, f32[264,256]{1,0:T(8,128)S(1)}) custom-call(f32[1,8]{1,0:T(1,128)} %bitcast.13, bf16[16,32]{1,0:T(8,128)(2,1)} %assign.7, bf16[4096,128]{1,0:T(8,128)(2,1)} %bitcast.16, bf16[4096,128]{1,0:T(8,128)(2,1)} %bitcast.19, bf16[4096,384]{1,0:T(8,128)(2,1)S(1)} %get-tuple-element.27.rows_in), custom_call_target="tpu_custom_call" | custom-call | tf_op jit(solution)/shard_map/cross/pallas_call | solution.py:420
  47.0 2.9 %all-to-all-done.1 = f32[16,33,128]{2,1,0:T(8,128)} async-done(((f32[16,33,128]{2,1,0:T(8,128)}), f32[16,33,128]{2,1,0:T(8,128)}, u32[]{:S(2)}, u32[]{:S(2)}) %all-to-all-start.1) | async-done | bytes 270368 | tf_op jit(solution)/shard_map/all_to_all | solution.py:362
  49.9 1.0 reduce_sum.37
  50.9 3.7 %all-gather.1.pool = f32[2,33,128]{2,1,0:T(8,128)S(1)} all-gather(f32[1,33,128]{2,1,0:T(8,128)S(1)} %bitcast.21), channel_id=2, replica_groups=mesh['z4'=2,'z2'=2,'z1'=2,'y'=4,'zh'=2,'x'=4,'core'=2] {'core'}, dimensions={0}, use_global_device_ids=true | all-gather | bytes 50688 | tf_op jit(solution)/shard_map/all_gather | solution.py:368
  54.6 0.0 copy-done
  54.6 0.0 copy-done.1
  54.6 0.0 copy-done.2
  54.6 0.0 copy-done.3
  54.6 0.0 copy-done.4
  54.6 6.0 %back.1 = (bf16[4096,256]{1,0:T(8,128)(2,1)}, bf16[256,128]{1,0:T(8,128)(2,1)S(1)}, f32[512,128]{1,0:T(8,128)S(1)}) custom-call(f32[1,8]{1,0:T(1,128)S(1)} %bitcast.14, bf16[16,32]{1,0:T(8,128)(2,1)S(1)} %copy-done, bf16[16,16]{1,0:T(8,128)(2,1)S(1)} %copy-done.2, bf16[16,16]{1,0:T(8,128)(2,1)S(1)} %copy-done.3, bf16[16,16]{1,0:T(8,128)(2,1)S(1)} %copy-done.4, ...), custom_call_target="tpu_custom_call" | custom-call | tf_op jit(solution)/shard_map/back/pallas_call | solution.py:439
  60.7 14.0 %all_to_all.26 = f32[64,8,128]{2,1,0:T(8,128)S(1)} all-to-all(f32[64,8,128]{2,1,0:T(8,128)S(1)} %bitcast.11), channel_id=1, replica_groups=mesh['z4'=2,'z2'=2,'z1'=2,'y'=4,'zh'=2,'x'=4,'core'=2] {'z1','y','x','co..., dimensions={0} | all-to-all | bytes 524288 | tf_op jit(solution)/shard_map/all_to_all | solution.py:373
  74.7 0.1 reduce_sum.38
  74.8 15.4 %all_to_all.27 = f32[8,8,128]{2,1,0:T(8,128)S(1)} all-to-all(f32[8,8,128]{2,1,0:T(8,128)S(1)} %broadcast_in_dim.32), channel_id=1, replica_groups=mesh['z4'=2,'z2'=2,'z1'=2,'y'=4,'zh'=2,'x'=4,'core'=2] {'z4','z2','zh'}, dimensions={0} | all-to-all | bytes 65536 | tf_op jit(solution)/shard_map/all_to_all | solution.py:362
  90.2 0.7 broadcast_in_dim.33
  91.0 6.1 %all-to-all-start.4 = ((f32[64,8,128]{2,1,0:T(8,128)}), f32[64,8,128]{2,1,0:T(8,128)S(1)}, u32[]{:S(2)}, u32[]{:S(2)}) async-start(f32[64,8,128]{2,1,0:T(8,128)} %broadcast_in_dim.33), calls=%async_computation.4 | async-start | bytes 524288 | tf_op jit(solution)/shard_map/all_to_all | solution.py:362
  97.1 5.6 %sense.1 = f32[4096,128]{1,0:T(8,128)} custom-call(bf16[128,128]{1,0:T(8,128)(2,1)} %hidden.3, bf16[128,128]{1,0:T(8,128)(2,1)} %aggregate.3, bf16[16,32]{1,0:T(8,128)(2,1)} %assign.7, bf16[256,128]{1,0:T(8,128)(2,1)S(1)} %get-tuple-element.30.numers, bf16[4096,256]{1,0:T(8,128)(2,1)} %get-tuple-element.31.score, f32[4096,256]{1,0:T(8,128)} %get-tuple-element.29.probs_hbm.probs), custom_call_target="tpu_custom_call" | custom-call | tf_op jit(solution)/shard_map/sense/pallas_call | solution.py:471
  102.7 4.1 %all-to-all-done.4 = f32[64,8,128]{2,1,0:T(8,128)S(1)} async-done(((f32[64,8,128]{2,1,0:T(8,128)}), f32[64,8,128]{2,1,0:T(8,128)S(1)}, u32[]{:S(2)}, u32[]{:S(2)}) %all-to-all-start.4) | async-done | bytes 262176 | tf_op jit(solution)/shard_map/all_to_all | solution.py:362
  106.8 0.7 split.1
  (3 shorter events, 0.0 us)
Async XLA Ops:
  34.7 19.9 %copy-start = (bf16[16,32]{1,0:T(8,128)(2,1)S(1)}, bf16[16,32]{1,0:T(8,128)(2,1)}, u32[]{:S(2)}) copy-start(bf16[16,32]{1,0:T(8,128)(2,1)} %assign.7) | copy-start | bytes 3076
  34.7 19.9 %copy-start.1 = (f32[8]{0:T(128)S(1)}, f32[8]{0:T(128)}, u32[]{:S(2)}) copy-start(f32[8]{0:T(128)} %param.17) | copy-start | bytes 100
  34.7 19.9 %copy-start.2 = (bf16[16,16]{1,0:T(8,128)(2,1)S(1)}, bf16[16,16]{1,0:T(8,128)(2,1)}, u32[]{:S(2)}) copy-start(bf16[16,16]{1,0:T(8,128)(2,1)} %ask.1) | copy-start | bytes 1540
  34.7 19.9 %copy-start.3 = (bf16[16,16]{1,0:T(8,128)(2,1)S(1)}, bf16[16,16]{1,0:T(8,128)(2,1)}, u32[]{:S(2)}) copy-start(bf16[16,16]{1,0:T(8,128)(2,1)} %look.1) | copy-start | bytes 1540
  34.7 19.9 %copy-start.4 = (bf16[16,16]{1,0:T(8,128)(2,1)S(1)}, bf16[16,16]{1,0:T(8,128)(2,1)}, u32[]{:S(2)}) copy-start(bf16[16,16]{1,0:T(8,128)(2,1)} %content.1) | copy-start | bytes 1540
  34.8 15.1 %all-to-all-start.1 = ((f32[16,33,128]{2,1,0:T(8,128)}), f32[16,33,128]{2,1,0:T(8,128)}, u32[]{:S(2)}, u32[]{:S(2)}) async-start(f32[16,33,128]{2,1,0:T(8,128)} %broadcast_in_dim.14), calls=%async_computation.1 | async-start | bytes 655360 | tf_op jit(solution)/shard_map/all_to_all | solution.py:362
  91.0 15.8 %all-to-all-start.4 = ((f32[64,8,128]{2,1,0:T(8,128)}), f32[64,8,128]{2,1,0:T(8,128)S(1)}, u32[]{:S(2)}, u32[]{:S(2)}) async-start(f32[64,8,128]{2,1,0:T(8,128)} %broadcast_in_dim.33), calls=%async_computation.4 | async-start | bytes 524288 | tf_op jit(solution)/shard_map/all_to_all | solution.py:362

commit v5 on v4

--- a/solution.py
+++ b/solution.py
@@ -362,17 +362,22 @@
     return lax.all_to_all(sent, axes, 0, 0, tiled=True)
 
 
-def sum_over_nodes(sent):
+def sum_over_nodes(sent, beside):
     part = jnp.sum(lax.all_to_all(sent, ("zh", "core"), 0, 0, tiled=True), 0)
+    part, beside = lax.optimization_barrier((part, beside))
     part = jnp.sum(exchange(part, ("y", "x"), 16), 0)
-    return lax.all_gather(part, "core", axis=0, tiled=False)
-
-
-def sum_over_all(sent):
+    return lax.all_gather(part, "core", axis=0, tiled=False), beside
+
+
+def scatter_sum(sent):
     sent = sent.reshape(64, GRAD_ROWS // 64, 128)
-    part = jnp.sum(lax.all_to_all(sent, BLOCK, 0, 0, tiled=True), 0)
+    return jnp.sum(lax.all_to_all(sent, BLOCK, 0, 0, tiled=True), 0)
+
+
+def gather_sum(part, beside):
     part = jnp.sum(exchange(part, COLUMN, 8), 0)
-    return exchange(part, BLOCK, 64).reshape(GRAD_ROWS, 128)
+    part, beside = lax.optimization_barrier((part, beside))
+    return exchange(part, BLOCK, 64).reshape(GRAD_ROWS, 128), beside
 
 
 def whole(shape):
@@ -513,16 +518,18 @@
         assignment_projection, softmax_sharpness[None], result_projection,
     )
     sharp = softmax_sharpness[None]
-    pool_sum = sum_over_nodes(pooled)
-    probs, crossed = cross(x, g, assignment_projection, sharp, rows)
+    beside = cross(x, g, assignment_projection, sharp, rows)
+    pool_sum, (probs, crossed) = sum_over_nodes(pooled, beside)
     score, numers, grads = back(
         pool_sum, crossed, x, assignment_projection, sharp, state_asking_map, state_lookup_map,
         state_content_map, probs, rows,
     )
+    part, score = lax.optimization_barrier((scatter_sum(grads), score))
     nodes_out = sense(
         hidden_projection, aggregate_projection, assignment_projection, numers, score, probs
     )
-    mid, feat, bias, slices, heat, ask, look, content, result = split(sum_over_all(grads))
+    total, nodes_out = gather_sum(part, nodes_out)
+    mid, feat, bias, slices, heat, ask, look, content, result = split(total)
     return nodes_out[None], mid, feat, bias[0], slices, heat[0], ask, look, content, result
 
 

time: 108 us -> 109 us (level)
  blocking collectives: 61.6 us -> 48 us
  starting transfers between devices: 13 us -> 21.2 us
  waiting for transfers between devices: 7.03 us -> 12.6 us
    all_to_all x2 -> x1, blocking collectives: 42.4 us -> 13.8 us  [scatter_sum(): return jnp.sum(lax.all_to_all(sent, BLOCK, 0, 0, tiled=True), 0)]
    all_to_all x0 -> x1, starting transfers between devices: none -> 16.6 us  [sum_over_nodes(): part = jnp.sum(lax.all_to_all(sent, ('zh', 'core'), 0, 0, tiled=True), 0)]
    all_to_all x1 -> x2, blocking collectives: 15.4 us -> 30.4 us  [exchange(): return lax.all_to_all(sent, axes, 0, 0, tiled=True)]
    all_to_all x2 -> x1, starting transfers between devices: 13 us -> 4.58 us  [exchange(): return lax.all_to_all(sent, axes, 0, 0, tiled=True)]
    all_to_all x0 -> x1, waiting for transfers between devices: none -> 6.8 us  [sum_over_nodes(): part = jnp.sum(lax.all_to_all(sent, ('zh', 'core'), 0, 0, tiled=True), 0)]
    all_to_all x2 -> x1, waiting for transfers between devices: 7.03 us -> 5.77 us  [exchange(): return lax.all_to_all(sent, axes, 0, 0, tiled=True)]
where the time goes in v5:
time: 109 us; the launch traced here: 108 us
  blocking collectives  48 us (44%)
  Pallas kernels  23.2 us (21%)
  starting transfers between devices  21.2 us (19%)
  waiting for transfers between devices  12.6 us (12%)
  other arithmetic  1.98 us (2%)
    all_to_all x2, blocking collectives, exchange(): return lax.all_to_all(sent, axes, 0, 0, tiled=True)  30.4 us
    all_to_all x1, starting transfers between devices, sum_over_nodes(): part = jnp.sum(lax.all_to_all(sent, ('zh', 'core'), 0, 0, tiled=True), 0)  16.6 us
    all_to_all x1, blocking collectives, scatter_sum(): return jnp.sum(lax.all_to_all(sent, BLOCK, 0, 0, tiled=True), 0)  13.8 us
    all_to_all x1, waiting for transfers between devices, sum_over_nodes(): part = jnp.sum(lax.all_to_all(sent, ('zh', 'core'), 0, 0, tiled=True), 0)  6.8 us
    pallas_call x1, Pallas kernels, back(): pl.pallas_call(back_kernel, grid=(nodes // TILE,), in_specs=[whole((1, HE...  6.04 us
    all_to_all x1, waiting for transfers between devices, exchange(): return lax.all_to_all(sent, axes, 0, 0, tiled=True)  5.77 us
    pallas_call x1, Pallas kernels, sense(): pl.pallas_call(sense_kernel, grid=(nodes // TILE,), in_specs=[square, squ...  5.61 us
    pallas_call x1, Pallas kernels, pool(): pl.pallas_call(pool_kernel, grid=(nodes // TILE,), in_specs=[whole((1, HE...  5.54 us
  transfers between devices with their start and end apart: 2, of which 2 were waited for; matrix products, arithmetic and copies ran while one was open for 0% of the time, Pallas kernels for 10%

profile of v5, /device:TPU:1, one launch (start us, length us, event | category | flops | bytes accessed | tf_op | source)
XLA Modules:
  0.0 108.3 jit_solution(6754895984311505876)
XLA Ops:
  0.6 5.5 %pool.1 = (bf16[4096,384]{1,0:T(8,128)(2,1)S(1)}, f32[4,33,128]{2,1,0:T(8,128)}) custom-call(f32[1,8]{1,0:T(1,128)} %bitcast.12, bf16[4096,128]{1,0:T(8,128)(2,1)} %bitcast.15, bf16[4096,128]{1,0:T(8,128)(2,1)} %bitcast.18, bf16[128,128]{1,0:T(8,128)(2,1)} %hidden.3, bf16[128,128]{1,0:T(8,128)(2,1)} %aggregate.3, f32[1,128]{1,0:T(1,128)} %bitcast.22, ...), custom_call_target="tpu_custom_call" | custom-call | tf_op jit(solution)/shard_map/pool/pallas_call | solution.py:401
  6.2 16.6 %all-to-all-start = ((f32[4,33,128]{2,1,0:T(8,128)}), f32[4,33,128]{2,1,0:T(8,128)}, u32[]{:S(2)}, u32[]{:S(2)}) async-start(f32[4,33,128]{2,1,0:T(8,128)} %get-tuple-element.33), calls=%async_computation | async-start | bytes 163840 | tf_op jit(solution)/shard_map/all_to_all | solution.py:366
  22.8 0.0 copy-start
  22.8 0.0 copy-start.1
  22.8 0.0 copy-start.2
  22.8 0.0 copy-start.3
  22.8 0.0 copy-start.4
  22.8 5.3 %cross.1 = (f32[4096,256]{1,0:T(8,128)}, f32[264,256]{1,0:T(8,128)S(1)}) custom-call(f32[1,8]{1,0:T(1,128)} %bitcast.13, bf16[16,32]{1,0:T(8,128)(2,1)} %assign.7, bf16[4096,128]{1,0:T(8,128)(2,1)} %bitcast.16, bf16[4096,128]{1,0:T(8,128)(2,1)} %bitcast.19, bf16[4096,384]{1,0:T(8,128)(2,1)S(1)} %get-tuple-element.34.rows_in), custom_call_target="tpu_custom_call" | custom-call | tf_op jit(solution)/shard_map/cross/pallas_call | solution.py:425
  28.1 6.8 %all-to-all-done = f32[4,33,128]{2,1,0:T(8,128)} async-done(((f32[4,33,128]{2,1,0:T(8,128)}), f32[4,33,128]{2,1,0:T(8,128)}, u32[]{:S(2)}, u32[]{:S(2)}) %all-to-all-start) | async-done | bytes 67616 | tf_op jit(solution)/shard_map/all_to_all | solution.py:366
  34.9 0.9 reduce_sum.36
  35.8 14.8 %all_to_all.25 = f32[16,33,128]{2,1,0:T(8,128)} all-to-all(f32[16,33,128]{2,1,0:T(8,128)S(1)} %broadcast_in_dim.14), channel_id=1, replica_groups=mesh['z4'=2,'z2'=2,'z1'=2,'y'=4,'zh'=2,'x'=4,'core'=2] {'y','x'}, dimensions={0} | all-to-all | bytes 540672 | tf_op jit(solution)/shard_map/all_to_all | solution.py:362
  50.6 1.0 reduce_sum.37
  51.6 3.7 %all-gather.1.pool = f32[2,33,128]{2,1,0:T(8,128)S(1)} all-gather(f32[1,33,128]{2,1,0:T(8,128)S(1)} %bitcast.21), channel_id=2, replica_groups=mesh['z4'=2,'z2'=2,'z1'=2,'y'=4,'zh'=2,'x'=4,'core'=2] {'core'}, dimensions={0}, use_global_device_ids=true | all-gather | bytes 50688 | tf_op jit(solution)/shard_map/all_gather | solution.py:369
  55.3 0.0 copy-done
  55.3 0.0 copy-done.1
  55.3 0.0 copy-done.2
  55.3 0.0 copy-done.3
  55.3 0.0 copy-done.4
  55.3 6.0 %back.1 = (bf16[4096,256]{1,0:T(8,128)(2,1)}, bf16[256,128]{1,0:T(8,128)(2,1)S(1)}, f32[512,128]{1,0:T(8,128)S(1)}) custom-call(f32[1,8]{1,0:T(1,128)S(1)} %bitcast.14, bf16[16,32]{1,0:T(8,128)(2,1)S(1)} %copy-done, bf16[16,16]{1,0:T(8,128)(2,1)S(1)} %copy-done.2, bf16[16,16]{1,0:T(8,128)(2,1)S(1)} %copy-done.3, bf16[16,16]{1,0:T(8,128)(2,1)S(1)} %copy-done.4, ...), custom_call_target="tpu_custom_call" | custom-call | tf_op jit(solution)/shard_map/back/pallas_call | solution.py:444
  61.4 13.8 %all_to_all.26 = f32[64,8,128]{2,1,0:T(8,128)S(1)} all-to-all(f32[64,8,128]{2,1,0:T(8,128)S(1)} %bitcast.11), channel_id=1, replica_groups=mesh['z4'=2,'z2'=2,'z1'=2,'y'=4,'zh'=2,'x'=4,'core'=2] {'z1','y','x','co..., dimensions={0} | all-to-all | bytes 524288 | tf_op jit(solution)/shard_map/all_to_all | solution.py:374
  75.2 0.1 reduce_sum.38
  75.3 0.6 broadcast_in_dim.15
  75.9 4.6 %all-to-all-start.3 = ((f32[8,8,128]{2,1,0:T(8,128)}), f32[8,8,128]{2,1,0:T(8,128)S(1)}, u32[]{:S(2)}, u32[]{:S(2)}) async-start(f32[8,8,128]{2,1,0:T(8,128)} %broadcast_in_dim.15), calls=%async_computation.3 | async-start | bytes 65536 | tf_op jit(solution)/shard_map/all_to_all | solution.py:362
  80.5 5.6 %sense.1 = f32[4096,128]{1,0:T(8,128)} custom-call(bf16[128,128]{1,0:T(8,128)(2,1)} %hidden.3, bf16[128,128]{1,0:T(8,128)(2,1)} %aggregate.3, bf16[16,32]{1,0:T(8,128)(2,1)} %assign.7, bf16[256,128]{1,0:T(8,128)(2,1)S(1)} %get-tuple-element.43.numers, bf16[4096,256]{1,0:T(8,128)(2,1)} %get-tuple-element.44.score, f32[4096,256]{1,0:T(8,128)} %get-tuple-element.39.probs_hbm.probs), custom_call_target="tpu_custom_call" | custom-call | tf_op jit(solution)/shard_map/sense/pallas_call | solution.py:476
  86.1 5.8 %all-to-all-done.3 = f32[8,8,128]{2,1,0:T(8,128)S(1)} async-done(((f32[8,8,128]{2,1,0:T(8,128)}), f32[8,8,128]{2,1,0:T(8,128)S(1)}, u32[]{:S(2)}, u32[]{:S(2)}) %all-to-all-start.3) | async-done | bytes 32800 | tf_op jit(solution)/shard_map/all_to_all | solution.py:362
  91.9 15.6 %all_to_all.27 = f32[64,8,128]{2,1,0:T(8,128)S(1)} all-to-all(f32[64,8,128]{2,1,0:T(8,128)S(1)} %broadcast_in_dim.33), channel_id=1, replica_groups=mesh['z4'=2,'z2'=2,'z1'=2,'y'=4,'zh'=2,'x'=4,'core'=2] {'z1','y','x','co..., dimensions={0} | all-to-all | bytes 524288 | tf_op jit(solution)/shard_map/all_to_all | solution.py:362
  107.5 0.7 split.1
  (3 shorter events, 0.1 us)
Async XLA Ops:
  6.2 28.7 %all-to-all-start = ((f32[4,33,128]{2,1,0:T(8,128)}), f32[4,33,128]{2,1,0:T(8,128)}, u32[]{:S(2)}, u32[]{:S(2)}) async-start(f32[4,33,128]{2,1,0:T(8,128)} %get-tuple-element.33), calls=%async_computation | async-start | bytes 163840 | tf_op jit(solution)/shard_map/all_to_all | solution.py:366
  22.8 32.5 %copy-start = (bf16[16,32]{1,0:T(8,128)(2,1)S(1)}, bf16[16,32]{1,0:T(8,128)(2,1)}, u32[]{:S(2)}) copy-start(bf16[16,32]{1,0:T(8,128)(2,1)} %assign.7) | copy-start | bytes 3076
  22.8 32.5 %copy-start.1 = (f32[8]{0:T(128)S(1)}, f32[8]{0:T(128)}, u32[]{:S(2)}) copy-start(f32[8]{0:T(128)} %param.17) | copy-start | bytes 100
  22.8 32.5 %copy-start.2 = (bf16[16,16]{1,0:T(8,128)(2,1)S(1)}, bf16[16,16]{1,0:T(8,128)(2,1)}, u32[]{:S(2)}) copy-start(bf16[16,16]{1,0:T(8,128)(2,1)} %ask.1) | copy-start | bytes 1540
  22.8 32.5 %copy-start.3 = (bf16[16,16]{1,0:T(8,128)(2,1)S(1)}, bf16[16,16]{1,0:T(8,128)(2,1)}, u32[]{:S(2)}) copy-start(bf16[16,16]{1,0:T(8,128)(2,1)} %look.1) | copy-start | bytes 1540
  22.8 32.5 %copy-start.4 = (bf16[16,16]{1,0:T(8,128)(2,1)S(1)}, bf16[16,16]{1,0:T(8,128)(2,1)}, u32[]{:S(2)}) copy-start(bf16[16,16]{1,0:T(8,128)(2,1)} %content.1) | copy-start | bytes 1540
  75.9 16.0 %all-to-all-start.3 = ((f32[8,8,128]{2,1,0:T(8,128)}), f32[8,8,128]{2,1,0:T(8,128)S(1)}, u32[]{:S(2)}, u32[]{:S(2)}) async-start(f32[8,8,128]{2,1,0:T(8,128)} %broadcast_in_dim.15), calls=%async_computation.3 | async-start | bytes 65536 | tf_op jit(solution)/shard_map/all_to_all | solution.py:362

commit v6 on v4

--- a/solution.py
+++ b/solution.py
@@ -168,29 +168,53 @@
 
 
 def cross_kernel(
-    sharp, assign, x, g, rows_in, probs_out, cross_out, assign_wide, scale, ones, mass,
+    sharp, assign, rows_in, x_hbm, g_hbm, cross_out, probs_hbm,
+    pairs, probs_all, assign_wide, scale, ones, mass, sems,
 ):
     step = pl.program_id(0)
+    tiles = probs_hbm.shape[0] // TILE
+
+    def moves(i):
+        t = slice(i * TILE, (i + 1) * TILE)
+        return (
+            pltpu.make_async_copy(x_hbm.at[t], pairs.at[t, :WIDTH], sems.at[3 * i]),
+            pltpu.make_async_copy(g_hbm.at[t], pairs.at[t, WIDTH:], sems.at[3 * i + 1]),
+            pltpu.make_async_copy(probs_all.at[t], probs_hbm.at[t], sems.at[3 * i + 2]),
+        )
 
     @pl.when(step == 0)
     def _():
+        for i in range(tiles):
+            for copy in moves(i)[:2]:
+                copy.start()
         assign_wide[...] = block_slices(assign[...]).astype(BF16)
         scale[...] = sharpness_row(sharp[...])
         ones[...] = head_sums()
         cross_out[...] = jnp.zeros_like(cross_out)
         mass[...] = jnp.zeros_like(mass)
 
+    here = pl.ds(pl.multiple_of(step * TILE, TILE), TILE)
     expon = jnp.exp(dot(rows_in[:, :WIDTH], assign_wide[...]) * scale[...])
     probs = expon * both_halves(1.0 / group_sum(expon, ones[...]))
-    probs_out[...] = probs
+    probs_all[here] = probs
+    for i in range(tiles):
+
+        @pl.when(step == i)
+        def _(i=i):
+            moves(i)[2].start()
+            for copy in moves(i)[:2]:
+                copy.wait()
+
     half = probs.astype(BF16)
     mass[...] += fold_rows(half.astype(F32), 8)
-    cross_out[:LANES] += dot(half, jnp.concatenate([x[...], g[...]], 1), 0, 0)
-
-    @pl.when(step == pl.num_programs(0) - 1)
+    cross_out[:LANES] += dot(half, pairs[here], 0, 0)
+
+    @pl.when(step == tiles - 1)
     def _():
         total = jnp.sum(mass[...], 0, keepdims=True)
         cross_out[LANES:] = jnp.broadcast_to(total, (8, LANES))
+        for i in range(tiles):
+            moves(i)[2].wait()
 
 
 def attend_terms(pool, ask, look, content, ones):
@@ -333,12 +357,18 @@
             sends(i).wait()
 
 
-def sense_kernel(hidden, aggregate, assign, numers, score, probs, sense_out):
-    weights = jnp.concatenate([hidden[...], aggregate[...]], 1)
-    assign_wide = block_slices(assign[...]).astype(BF16)
-    mid_back = dot(score[...], assign_wide, 1, 1).astype(BF16)
+def sense_kernel(
+    hidden, aggregate, assign, numers, score, probs, sense_out, weights, assign_wide,
+):
+    @pl.when(pl.program_id(0) == 0)
+    def _():
+        weights[:, :WIDTH] = hidden[...]
+        weights[:, WIDTH:] = aggregate[...]
+        assign_wide[...] = block_slices(assign[...]).astype(BF16)
+
+    mid_back = dot(score[...], assign_wide[...], 1, 1).astype(BF16)
     feat_back = dot(probs[...].astype(BF16), numers[...]).astype(BF16)
-    sense_out[...] = dot(jnp.concatenate([mid_back, feat_back], 1), weights, 1, 1)
+    sense_out[...] = dot(jnp.concatenate([mid_back, feat_back], 1), weights[...], 1, 1)
 
 
 def split_kernel(
@@ -417,21 +447,22 @@
 
 def cross(x, g, assign, sharp, rows):
     nodes = x.shape[0]
+    raw = pl.BlockSpec(memory_space=pltpu.HBM)
     return pl.pallas_call(
         cross_kernel,
         grid=(nodes // TILE,),
-        in_specs=[
-            whole((1, HEADS)), whole((D, SLICES)), tiled(WIDTH), tiled(WIDTH), tiled(3 * WIDTH),
-        ],
-        out_specs=[tiled(LANES), whole((LANES + 8, LANES))],
-        out_shape=[pltpu.HBM((nodes, LANES), F32), shape((LANES + 8, LANES))],
+        in_specs=[whole((1, HEADS)), whole((D, SLICES)), tiled(3 * WIDTH), raw, raw],
+        out_specs=[whole((LANES + 8, LANES)), raw],
+        out_shape=[shape((LANES + 8, LANES)), pltpu.HBM((nodes, LANES), F32)],
         scratch_shapes=[
+            pltpu.VMEM((nodes, LANES), BF16), pltpu.VMEM((nodes, LANES), F32),
             pltpu.VMEM((WIDTH, LANES), BF16), pltpu.VMEM((1, LANES), F32),
             pltpu.VMEM((LANES, WIDTH), BF16), pltpu.VMEM((8, LANES), F32),
+            pltpu.SemaphoreType.DMA((3 * (nodes // TILE),)),
         ],
         compiler_params=pltpu.CompilerParams(vmem_limit_bytes=40 << 20),
         name="cross",
-    )(hbm(sharp), hbm(assign), hbm(x), hbm(g), rows)
+    )(hbm(sharp), hbm(assign), rows, hbm(x), hbm(g))
 
 
 def back(pool_sum, crossed, x, assign, sharp, ask, look, content, probs, rows):
@@ -476,6 +507,7 @@
         ],
         out_specs=tiled(WIDTH),
         out_shape=pltpu.HBM((nodes, WIDTH), F32),
+        scratch_shapes=[pltpu.VMEM((WIDTH, LANES), BF16), pltpu.VMEM((WIDTH, LANES), BF16)],
         compiler_params=pltpu.CompilerParams(vmem_limit_bytes=40 << 20),
         name="sense",
     )(*[hbm(a) for a in (hidden, aggregate, assign)], numers, hbm(score), hbm(probs))
@@ -514,7 +546,7 @@
     )
     sharp = softmax_sharpness[None]
     pool_sum = sum_over_nodes(pooled)
-    probs, crossed = cross(x, g, assignment_projection, sharp, rows)
+    crossed, probs = cross(x, g, assignment_projection, sharp, rows)
     score, numers, grads = back(
         pool_sum, crossed, x, assignment_projection, sharp, state_asking_map, state_lookup_map,
         state_content_map, probs, rows,

time: 108 us -> 108 us (level)
  no operation moved by 1% of the time
where the time goes in v6:
time: 108 us; the launch traced here: 107 us
  blocking collectives  61.4 us (57%)
  Pallas kernels  22.1 us (20%)
  starting transfers between devices  13 us (12%)
  waiting for transfers between devices  7.43 us (7%)
  local copies, waits for them, and re-layouts  1.51 us (1%)
  other arithmetic  1.09 us (1%)
    all_to_all x1, blocking collectives, sum_over_nodes(): part = jnp.sum(lax.all_to_all(sent, ('zh', 'core'), 0, 0, tiled=True), 0)  28.4 us
    all_to_all x1, blocking collectives, exchange(): return lax.all_to_all(sent, axes, 0, 0, tiled=True)  15.5 us
    all_to_all x1, blocking collectives, sum_over_all(): part = jnp.sum(lax.all_to_all(sent, BLOCK, 0, 0, tiled=True), 0)  13.9 us
    all_to_all x2, starting transfers between devices, exchange(): return lax.all_to_all(sent, axes, 0, 0, tiled=True)  13 us
    all_to_all x2, waiting for transfers between devices, exchange(): return lax.all_to_all(sent, axes, 0, 0, tiled=True)  7.43 us
    pallas_call x1, Pallas kernels, back(): pl.pallas_call(back_kernel, grid=(nodes // TILE,), in_specs=[whole((1, HE...  6.04 us
    pallas_call x1, Pallas kernels, sense(): pl.pallas_call(sense_kernel, grid=(nodes // TILE,), in_specs=[square, squ...  5.44 us
    pallas_call x1, Pallas kernels, cross(): pl.pallas_call(cross_kernel, grid=(nodes // TILE,), in_specs=[whole((1, H...  5.02 us
  transfers between devices with their start and end apart: 2, of which 2 were waited for; matrix products, arithmetic and copies ran while one was open for 0% of the time, Pallas kernels for 10%

profile of v6, /device:TPU:1, one launch (start us, length us, event | category | flops | bytes accessed | tf_op | source)
XLA Modules:
  0.0 107.4 jit_solution(10841663787281601195)
XLA Ops:
  0.6 4.9 %pool.1 = (bf16[4096,384]{1,0:T(8,128)(2,1)S(1)}, f32[4,33,128]{2,1,0:T(8,128)S(1)}) custom-call(f32[1,8]{1,0:T(1,128)} %bitcast.12, bf16[4096,128]{1,0:T(8,128)(2,1)} %bitcast.15, bf16[4096,128]{1,0:T(8,128)(2,1)} %bitcast.18, bf16[128,128]{1,0:T(8,128)(2,1)} %hidden.3, bf16[128,128]{1,0:T(8,128)(2,1)} %aggregate.3, f32[1,128]{1,0:T(1,128)} %bitcast.22, ...), custom_call_target="tpu_custom_call" | custom-call | tf_op jit(solution)/shard_map/pool/pallas_call | solution.py:426
  5.6 28.4 %all_to_all.25 = f32[4,33,128]{2,1,0:T(8,128)S(1)} all-to-all(f32[4,33,128]{2,1,0:T(8,128)S(1)} %get-tuple-element.26), channel_id=1, replica_groups=mesh['z4'=2,'z2'=2,'z1'=2,'y'=4,'zh'=2,'x'=4,'core'=2] {'zh','core'}, dimensions={0} | all-to-all | bytes 135168 | tf_op jit(solution)/shard_map/all_to_all | solution.py:396
  34.0 0.7 broadcast_in_dim.14
  34.7 0.0 copy-start
  34.7 0.0 copy-start.1
  34.7 0.0 copy-start.2
  34.7 0.0 copy-start.3
  34.7 0.0 copy-start.4
  34.8 6.9 %all-to-all-start.1 = ((f32[16,33,128]{2,1,0:T(8,128)}), f32[16,33,128]{2,1,0:T(8,128)}, u32[]{:S(2)}, u32[]{:S(2)}) async-start(f32[16,33,128]{2,1,0:T(8,128)} %broadcast_in_dim.14), calls=%async_computation.1 | async-start | bytes 655360 | tf_op jit(solution)/shard_map/all_to_all | solution.py:392
  41.7 5.0 %cross.1 = (f32[264,256]{1,0:T(8,128)S(1)}, f32[4096,256]{1,0:T(8,128)}) custom-call(f32[1,8]{1,0:T(1,128)} %bitcast.13, bf16[16,32]{1,0:T(8,128)(2,1)} %assign.7, bf16[4096,384]{1,0:T(8,128)(2,1)S(1)} %get-tuple-element.27.rows_in, bf16[4096,128]{1,0:T(8,128)(2,1)} %bitcast.16, bf16[4096,128]{1,0:T(8,128)(2,1)} %bitcast.19), custom_call_target="tpu_custom_call" | custom-call | tf_op jit(solution)/shard_map/cross/pallas_call | solution.py:451
  46.7 3.1 %all-to-all-done.1 = f32[16,33,128]{2,1,0:T(8,128)} async-done(((f32[16,33,128]{2,1,0:T(8,128)}), f32[16,33,128]{2,1,0:T(8,128)}, u32[]{:S(2)}, u32[]{:S(2)}) %all-to-all-start.1) | async-done | bytes 270368 | tf_op jit(solution)/shard_map/all_to_all | solution.py:392
  49.9 1.0 reduce_sum.37
  50.9 3.7 %all-gather.1.pool = f32[2,33,128]{2,1,0:T(8,128)S(1)} all-gather(f32[1,33,128]{2,1,0:T(8,128)S(1)} %bitcast.21), channel_id=2, replica_groups=mesh['z4'=2,'z2'=2,'z1'=2,'y'=4,'zh'=2,'x'=4,'core'=2] {'core'}, dimensions={0}, use_global_device_ids=true | all-gather | bytes 50688 | tf_op jit(solution)/shard_map/all_gather | solution.py:398
  54.6 0.0 copy-done
  54.6 0.0 copy-done.1
  54.6 0.0 copy-done.2
  54.6 0.0 copy-done.3
  54.6 0.0 copy-done.4
  54.6 6.0 %back.1 = (bf16[4096,256]{1,0:T(8,128)(2,1)}, bf16[256,128]{1,0:T(8,128)(2,1)S(1)}, f32[512,128]{1,0:T(8,128)S(1)}) custom-call(f32[1,8]{1,0:T(1,128)S(1)} %bitcast.14, bf16[16,32]{1,0:T(8,128)(2,1)S(1)} %copy-done, bf16[16,16]{1,0:T(8,128)(2,1)S(1)} %copy-done.2, bf16[16,16]{1,0:T(8,128)(2,1)S(1)} %copy-done.3, bf16[16,16]{1,0:T(8,128)(2,1)S(1)} %copy-done.4, ...), custom_call_target="tpu_custom_call" | custom-call | tf_op jit(solution)/shard_map/back/pallas_call | solution.py:470
  60.7 13.9 %all_to_all.26 = f32[64,8,128]{2,1,0:T(8,128)S(1)} all-to-all(f32[64,8,128]{2,1,0:T(8,128)S(1)} %bitcast.11), channel_id=1, replica_groups=mesh['z4'=2,'z2'=2,'z1'=2,'y'=4,'zh'=2,'x'=4,'core'=2] {'z1','y','x','co..., dimensions={0} | all-to-all | bytes 524288 | tf_op jit(solution)/shard_map/all_to_all | solution.py:403
  74.5 0.1 reduce_sum.38
  74.6 15.5 %all_to_all.27 = f32[8,8,128]{2,1,0:T(8,128)S(1)} all-to-all(f32[8,8,128]{2,1,0:T(8,128)S(1)} %broadcast_in_dim.32), channel_id=1, replica_groups=mesh['z4'=2,'z2'=2,'z1'=2,'y'=4,'zh'=2,'x'=4,'core'=2] {'z4','z2','zh'}, dimensions={0} | all-to-all | bytes 65536 | tf_op jit(solution)/shard_map/all_to_all | solution.py:392
  90.1 0.7 broadcast_in_dim.33
  90.8 6.1 %all-to-all-start.4 = ((f32[64,8,128]{2,1,0:T(8,128)}), f32[64,8,128]{2,1,0:T(8,128)S(1)}, u32[]{:S(2)}, u32[]{:S(2)}) async-start(f32[64,8,128]{2,1,0:T(8,128)} %broadcast_in_dim.33), calls=%async_computation.4 | async-start | bytes 524288 | tf_op jit(solution)/shard_map/all_to_all | solution.py:392
  96.9 5.4 %sense.1 = f32[4096,128]{1,0:T(8,128)} custom-call(bf16[128,128]{1,0:T(8,128)(2,1)} %hidden.3, bf16[128,128]{1,0:T(8,128)(2,1)} %aggregate.3, bf16[16,32]{1,0:T(8,128)(2,1)} %assign.7, bf16[256,128]{1,0:T(8,128)(2,1)S(1)} %get-tuple-element.30.numers, bf16[4096,256]{1,0:T(8,128)(2,1)} %get-tuple-element.31.score, f32[4096,256]{1,0:T(8,128)} %get-tuple-element.29.probs_hbm.probs), custom_call_target="tpu_custom_call" | custom-call | tf_op jit(solution)/shard_map/sense/pallas_call | solution.py:502
  102.4 4.3 %all-to-all-done.4 = f32[64,8,128]{2,1,0:T(8,128)S(1)} async-done(((f32[64,8,128]{2,1,0:T(8,128)}), f32[64,8,128]{2,1,0:T(8,128)S(1)}, u32[]{:S(2)}, u32[]{:S(2)}) %all-to-all-start.4) | async-done | bytes 262176 | tf_op jit(solution)/shard_map/all_to_all | solution.py:392
  106.6 0.7 split.1
  (3 shorter events, 0.0 us)
Async XLA Ops:
  34.7 19.9 %copy-start = (bf16[16,32]{1,0:T(8,128)(2,1)S(1)}, bf16[16,32]{1,0:T(8,128)(2,1)}, u32[]{:S(2)}) copy-start(bf16[16,32]{1,0:T(8,128)(2,1)} %assign.7) | copy-start | bytes 3076
  34.7 19.9 %copy-start.1 = (f32[8]{0:T(128)S(1)}, f32[8]{0:T(128)}, u32[]{:S(2)}) copy-start(f32[8]{0:T(128)} %param.17) | copy-start | bytes 100
  34.7 19.9 %copy-start.2 = (bf16[16,16]{1,0:T(8,128)(2,1)S(1)}, bf16[16,16]{1,0:T(8,128)(2,1)}, u32[]{:S(2)}) copy-start(bf16[16,16]{1,0:T(8,128)(2,1)} %ask.1) | copy-start | bytes 1540
  34.7 19.9 %copy-start.3 = (bf16[16,16]{1,0:T(8,128)(2,1)S(1)}, bf16[16,16]{1,0:T(8,128)(2,1)}, u32[]{:S(2)}) copy-start(bf16[16,16]{1,0:T(8,128)(2,1)} %look.1) | copy-start | bytes 1540
  34.7 19.9 %copy-start.4 = (bf16[16,16]{1,0:T(8,128)(2,1)S(1)}, bf16[16,16]{1,0:T(8,128)(2,1)}, u32[]{:S(2)}) copy-start(bf16[16,16]{1,0:T(8,128)(2,1)} %content.1) | copy-start | bytes 1540
  34.8 15.1 %all-to-all-start.1 = ((f32[16,33,128]{2,1,0:T(8,128)}), f32[16,33,128]{2,1,0:T(8,128)}, u32[]{:S(2)}, u32[]{:S(2)}) async-start(f32[16,33,128]{2,1,0:T(8,128)} %broadcast_in_dim.14), calls=%async_computation.1 | async-start | bytes 655360 | tf_op jit(solution)/shard_map/all_to_all | solution.py:392
  90.8 15.8 %all-to-all-start.4 = ((f32[64,8,128]{2,1,0:T(8,128)}), f32[64,8,128]{2,1,0:T(8,128)S(1)}, u32[]{:S(2)}, u32[]{:S(2)}) async-start(f32[64,8,128]{2,1,0:T(8,128)} %broadcast_in_dim.33), calls=%async_computation.4 | async-start | bytes 524288 | tf_op jit(solution)/shard_map/all_to_all | solution.py:392

commit v7 on v6

--- a/solution.py
+++ b/solution.py
@@ -15,8 +15,8 @@
 GRAD_ROWS = 512
 MEMBER = ("z4", "z2", "z1")
 NODE = ("y", "zh", "x", "core")
-BLOCK = ("z1", "y", "x", "core")
-COLUMN = ("z4", "z2", "zh")
+BLOCK = ("y", "x", "core")
+COLUMN = ("z4", "z2", "z1", "zh")
 F32 = jnp.float32
 BF16 = jnp.bfloat16
 
@@ -399,10 +399,10 @@
 
 
 def sum_over_all(sent):
-    sent = sent.reshape(64, GRAD_ROWS // 64, 128)
+    sent = sent.reshape(32, GRAD_ROWS // 32, 128)
     part = jnp.sum(lax.all_to_all(sent, BLOCK, 0, 0, tiled=True), 0)
-    part = jnp.sum(exchange(part, COLUMN, 8), 0)
-    return exchange(part, BLOCK, 64).reshape(GRAD_ROWS, 128)
+    part = jnp.sum(exchange(part, COLUMN, 16), 0)
+    return exchange(part, BLOCK, 32).reshape(GRAD_ROWS, 128)
 
 
 def whole(shape):

time: 108 us -> 108 us (level)
    all_to_all x1, blocking collectives: 15.5 us -> 18.1 us  [exchange(): return lax.all_to_all(sent, axes, 0, 0, tiled=True)]
    all_to_all x1, blocking collectives: 13.9 us -> 12.2 us  [sum_over_all(): part = jnp.sum(lax.all_to_all(sent, BLOCK, 0, 0, tiled=True), 0)]
where the time goes in v7:
time: 108 us
  blocking collectives  62.4 us (58%)
  Pallas kernels  22.1 us (20%)
  starting transfers between devices  13.2 us (12%)
  waiting for transfers between devices  6.71 us (6%)
  local copies, waits for them, and re-layouts  1.51 us (1%)
    all_to_all x1, blocking collectives, sum_over_nodes(): part = jnp.sum(lax.all_to_all(sent, ('zh', 'core'), 0, 0, tiled=True), 0)  28.4 us
    all_to_all x1, blocking collectives, exchange(): return lax.all_to_all(sent, axes, 0, 0, tiled=True)  18.1 us
    all_to_all x2, starting transfers between devices, exchange(): return lax.all_to_all(sent, axes, 0, 0, tiled=True)  13.2 us
    all_to_all x1, blocking collectives, sum_over_all(): part = jnp.sum(lax.all_to_all(sent, BLOCK, 0, 0, tiled=True), 0)  12.2 us
    all_to_all x2, waiting for transfers between devices, exchange(): return lax.all_to_all(sent, axes, 0, 0, tiled=True)  6.71 us
    pallas_call x1, Pallas kernels, back(): pl.pallas_call(back_kernel, grid=(nodes // TILE,), in_specs=[whole((1, HE...  6.04 us
    pallas_call x1, Pallas kernels, sense(): pl.pallas_call(sense_kernel, grid=(nodes // TILE,), in_specs=[square, squ...  5.44 us
    pallas_call x1, Pallas kernels, cross(): pl.pallas_call(cross_kernel, grid=(nodes // TILE,), in_specs=[whole((1, H...  5.02 us
  transfers between devices with their start and end apart: 2, of which 2 were waited for; matrix products, arithmetic and copies ran while one was open for 0% of the time, Pallas kernels for 10%

profile of v7, /device:TPU:1, one launch (start us, length us, event | category | flops | bytes accessed | tf_op | source)
XLA Modules:
  0.0 107.8 jit_solution(13789274597935231877)
XLA Ops:
  0.6 4.9 %pool.1 = (bf16[4096,384]{1,0:T(8,128)(2,1)S(1)}, f32[4,33,128]{2,1,0:T(8,128)S(1)}) custom-call(f32[1,8]{1,0:T(1,128)} %bitcast.12, bf16[4096,128]{1,0:T(8,128)(2,1)} %bitcast.15, bf16[4096,128]{1,0:T(8,128)(2,1)} %bitcast.18, bf16[128,128]{1,0:T(8,128)(2,1)} %hidden.3, bf16[128,128]{1,0:T(8,128)(2,1)} %aggregate.3, f32[1,128]{1,0:T(1,128)} %bitcast.22, ...), custom_call_target="tpu_custom_call" | custom-call | tf_op jit(solution)/shard_map/pool/pallas_call | solution.py:426
  5.6 28.4 %all_to_all.25 = f32[4,33,128]{2,1,0:T(8,128)S(1)} all-to-all(f32[4,33,128]{2,1,0:T(8,128)S(1)} %get-tuple-element.26), channel_id=1, replica_groups=mesh['z4'=2,'z2'=2,'z1'=2,'y'=4,'zh'=2,'x'=4,'core'=2] {'zh','core'}, dimensions={0} | all-to-all | bytes 135168 | tf_op jit(solution)/shard_map/all_to_all | solution.py:396
  34.0 0.7 broadcast_in_dim.14
  34.7 0.0 copy-start
  34.7 0.0 copy-start.1
  34.7 0.0 copy-start.2
  34.7 0.0 copy-start.3
  34.7 0.0 copy-start.4
  34.8 6.9 %all-to-all-start.1 = ((f32[16,33,128]{2,1,0:T(8,128)}), f32[16,33,128]{2,1,0:T(8,128)}, u32[]{:S(2)}, u32[]{:S(2)}) async-start(f32[16,33,128]{2,1,0:T(8,128)} %broadcast_in_dim.14), calls=%async_computation.1 | async-start | bytes 655360 | tf_op jit(solution)/shard_map/all_to_all | solution.py:392
  41.7 5.0 %cross.1 = (f32[264,256]{1,0:T(8,128)S(1)}, f32[4096,256]{1,0:T(8,128)}) custom-call(f32[1,8]{1,0:T(1,128)} %bitcast.13, bf16[16,32]{1,0:T(8,128)(2,1)} %assign.7, bf16[4096,384]{1,0:T(8,128)(2,1)S(1)} %get-tuple-element.27.rows_in, bf16[4096,128]{1,0:T(8,128)(2,1)} %bitcast.16, bf16[4096,128]{1,0:T(8,128)(2,1)} %bitcast.19), custom_call_target="tpu_custom_call" | custom-call | tf_op jit(solution)/shard_map/cross/pallas_call | solution.py:451
  46.7 3.1 %all-to-all-done.1 = f32[16,33,128]{2,1,0:T(8,128)} async-done(((f32[16,33,128]{2,1,0:T(8,128)}), f32[16,33,128]{2,1,0:T(8,128)}, u32[]{:S(2)}, u32[]{:S(2)}) %all-to-all-start.1) | async-done | bytes 270368 | tf_op jit(solution)/shard_map/all_to_all | solution.py:392
  49.9 1.0 reduce_sum.37
  50.9 3.7 %all-gather.1.pool = f32[2,33,128]{2,1,0:T(8,128)S(1)} all-gather(f32[1,33,128]{2,1,0:T(8,128)S(1)} %bitcast.21), channel_id=2, replica_groups=mesh['z4'=2,'z2'=2,'z1'=2,'y'=4,'zh'=2,'x'=4,'core'=2] {'core'}, dimensions={0}, use_global_device_ids=true | all-gather | bytes 50688 | tf_op jit(solution)/shard_map/all_gather | solution.py:398
  54.6 0.0 copy-done
  54.6 0.0 copy-done.1
  54.6 0.0 copy-done.2
  54.6 0.0 copy-done.3
  54.6 0.0 copy-done.4
  54.6 6.0 %back.1 = (bf16[4096,256]{1,0:T(8,128)(2,1)}, bf16[256,128]{1,0:T(8,128)(2,1)S(1)}, f32[512,128]{1,0:T(8,128)S(1)}) custom-call(f32[1,8]{1,0:T(1,128)S(1)} %bitcast.14, bf16[16,32]{1,0:T(8,128)(2,1)S(1)} %copy-done, bf16[16,16]{1,0:T(8,128)(2,1)S(1)} %copy-done.2, bf16[16,16]{1,0:T(8,128)(2,1)S(1)} %copy-done.3, bf16[16,16]{1,0:T(8,128)(2,1)S(1)} %copy-done.4, ...), custom_call_target="tpu_custom_call" | custom-call | tf_op jit(solution)/shard_map/back/pallas_call | solution.py:470
  60.7 12.2 %all_to_all.26 = f32[32,16,128]{2,1,0:T(8,128)S(1)} all-to-all(f32[32,16,128]{2,1,0:T(8,128)S(1)} %bitcast.11), channel_id=1, replica_groups=mesh['z4'=2,'z2'=2,'z1'=2,'y'=4,'zh'=2,'x'=4,'core'=2] {'y','x','core'}, dimensions={0} | all-to-all | bytes 524288 | tf_op jit(solution)/shard_map/all_to_all | solution.py:403
  72.9 18.1 %all_to_all.27 = f32[16,16,128]{2,1,0:T(8,128)S(1)} all-to-all(f32[16,16,128]{2,1,0:T(8,128)S(1)} %broadcast_in_dim.32), channel_id=1, replica_groups=mesh['z4'=2,'z2'=2,'z1'=2,'y'=4,'zh'=2,'x'=4,'core'=2] {'z4','z2','z1','..., dimensions={0} | all-to-all | bytes 262144 | tf_op jit(solution)/shard_map/all_to_all | solution.py:392
  91.0 0.7 broadcast_in_dim.33
  91.7 6.3 %all-to-all-start.4 = ((f32[32,16,128]{2,1,0:T(8,128)}), f32[32,16,128]{2,1,0:T(8,128)S(1)}, u32[]{:S(2)}, u32[]{:S(2)}) async-start(f32[32,16,128]{2,1,0:T(8,128)} %broadcast_in_dim.33), calls=%async_computation.4 | async-start | bytes 524288 | tf_op jit(solution)/shard_map/all_to_all | solution.py:392
  98.0 5.4 %sense.1 = f32[4096,128]{1,0:T(8,128)} custom-call(bf16[128,128]{1,0:T(8,128)(2,1)} %hidden.3, bf16[128,128]{1,0:T(8,128)(2,1)} %aggregate.3, bf16[16,32]{1,0:T(8,128)(2,1)} %assign.7, bf16[256,128]{1,0:T(8,128)(2,1)S(1)} %get-tuple-element.30.numers, bf16[4096,256]{1,0:T(8,128)(2,1)} %get-tuple-element.31.score, f32[4096,256]{1,0:T(8,128)} %get-tuple-element.29.probs_hbm.probs), custom_call_target="tpu_custom_call" | custom-call | tf_op jit(solution)/shard_map/sense/pallas_call | solution.py:502
  103.5 3.6 %all-to-all-done.4 = f32[32,16,128]{2,1,0:T(8,128)S(1)} async-done(((f32[32,16,128]{2,1,0:T(8,128)}), f32[32,16,128]{2,1,0:T(8,128)S(1)}, u32[]{:S(2)}, u32[]{:S(2)}) %all-to-all-start.4) | async-done | bytes 262176 | tf_op jit(solution)/shard_map/all_to_all | solution.py:392
  107.0 0.7 split.1
  (4 shorter events, 0.1 us)
Async XLA Ops:
  34.7 19.9 %copy-start = (bf16[16,32]{1,0:T(8,128)(2,1)S(1)}, bf16[16,32]{1,0:T(8,128)(2,1)}, u32[]{:S(2)}) copy-start(bf16[16,32]{1,0:T(8,128)(2,1)} %assign.7) | copy-start | bytes 3076
  34.7 19.9 %copy-start.1 = (f32[8]{0:T(128)S(1)}, f32[8]{0:T(128)}, u32[]{:S(2)}) copy-start(f32[8]{0:T(128)} %param.17) | copy-start | bytes 100
  34.7 19.9 %copy-start.2 = (bf16[16,16]{1,0:T(8,128)(2,1)S(1)}, bf16[16,16]{1,0:T(8,128)(2,1)}, u32[]{:S(2)}) copy-start(bf16[16,16]{1,0:T(8,128)(2,1)} %ask.1) | copy-start | bytes 1540
  34.7 19.9 %copy-start.3 = (bf16[16,16]{1,0:T(8,128)(2,1)S(1)}, bf16[16,16]{1,0:T(8,128)(2,1)}, u32[]{:S(2)}) copy-start(bf16[16,16]{1,0:T(8,128)(2,1)} %look.1) | copy-start | bytes 1540
  34.7 19.9 %copy-start.4 = (bf16[16,16]{1,0:T(8,128)(2,1)S(1)}, bf16[16,16]{1,0:T(8,128)(2,1)}, u32[]{:S(2)}) copy-start(bf16[16,16]{1,0:T(8,128)(2,1)} %content.1) | copy-start | bytes 1540
  34.8 15.1 %all-to-all-start.1 = ((f32[16,33,128]{2,1,0:T(8,128)}), f32[16,33,128]{2,1,0:T(8,128)}, u32[]{:S(2)}, u32[]{:S(2)}) async-start(f32[16,33,128]{2,1,0:T(8,128)} %broadcast_in_dim.14), calls=%async_computation.1 | async-start | bytes 655360 | tf_op jit(solution)/shard_map/all_to_all | solution.py:392
  91.7 15.3 %all-to-all-start.4 = ((f32[32,16,128]{2,1,0:T(8,128)}), f32[32,16,128]{2,1,0:T(8,128)S(1)}, u32[]{:S(2)}, u32[]{:S(2)}) async-start(f32[32,16,128]{2,1,0:T(8,128)} %broadcast_in_dim.33), calls=%async_computation.4 | async-start | bytes 524288 | tf_op jit(solution)/shard_map/all_to_all | solution.py:392
